TPU v7x, 32 devices: a whole 2x2x4 slice. The times are simulated.
32 devices in a mesh: dp: 2 (over core), fsdp: 16 (over z, y, x).
Axes of the slice: x: 2, y: 2, z: 4, core: 2. Of those that a mesh axis runs over, the one named last changes fastest.
Arguments:
- tokens: bfloat16 [8192, 1024], P(('dp', 'fsdp')), may hold values from -27 to 27
- attn_gain: bfloat16 [1024], P(('dp', 'fsdp')), may hold values from 0.5 to 1.5
- w_query: bfloat16 [1024, 1024], P(('dp', 'fsdp')), may hold values from -0.1875 to 0.1875
- w_key: bfloat16 [1024, 1024], P(('dp', 'fsdp')), may hold values from -0.1875 to 0.1875
- w_value: bfloat16 [1024, 1024], P(('dp', 'fsdp')), may hold values from -0.1875 to 0.1875
- w_gate: bfloat16 [1024, 1024], P(('dp', 'fsdp')), may hold values from -0.1875 to 0.1875
- w_output: bfloat16 [1024, 1024], P(('dp', 'fsdp')), may hold values from -0.75 to 0.75
- ffn_gain: bfloat16 [1024], P(('dp', 'fsdp')), may hold values from 0.5 to 1.5
- w_first: bfloat16 [1024, 2816], P(('dp', 'fsdp')), may hold values from -0.1875 to 0.1875
- w_second: bfloat16 [1024, 2816], P(('dp', 'fsdp')), may hold values from -0.1875 to 0.1875
- w_down: bfloat16 [2816, 1024], P(('dp', 'fsdp')), may hold values from -0.109375 to 0.109375
- cotangent: bfloat16 [8192, 1024], P(('dp', 'fsdp')), may hold values from -6 to 6
Outputs:
- block_out: bfloat16 [8192, 1024], P(('dp', 'fsdp'))
- tokens_grad: float32 [8192, 1024], P(('dp', 'fsdp'))
- attn_gain_grad: float32 [1024], P(('dp', 'fsdp'))
- w_query_grad: float32 [1024, 1024], P(('dp', 'fsdp'))
- w_key_grad: float32 [1024, 1024], P(('dp', 'fsdp'))
- w_value_grad: float32 [1024, 1024], P(('dp', 'fsdp'))
- w_gate_grad: float32 [1024, 1024], P(('dp', 'fsdp'))
- w_output_grad: float32 [1024, 1024], P(('dp', 'fsdp'))
- ffn_gain_grad: float32 [1024], P(('dp', 'fsdp'))
- w_first_grad: float32 [1024, 2816], P(('dp', 'fsdp'))
- w_second_grad: float32 [1024, 2816], P(('dp', 'fsdp'))
- w_down_grad: float32 [2816, 1024], P(('dp', 'fsdp'))
All inputs are finite; a program needn't handle non-finite values.
Results may differ from a plain program's by a relative error of at most 0.018.
Values may be sent and summed in bfloat16 or wider, within the bound.
A program may use at most 192 MiB of HBM per device.

v0:
```python
import jax
import jax.numpy as jnp
from jax import lax
from jax.sharding import PartitionSpec as P

D = 1024
HEADS = 16
HDIM = 64
FF = 2816
BLK = 64


EPS = 1e-06


def rms_scale(values, gain):
    return values * lax.rsqrt(jnp.mean(values * values, axis=-1, keepdims=True) + EPS) * gain


def gated(attended, gate_pre):
    return attended * jax.nn.silu(gate_pre)


def contract_rows(left, right):
    return lax.dot_general(
        left, right, (((0,), (0,)), ((), ())), preferred_element_type=jnp.float32
    )


def contract_cols(left, right):
    return lax.dot_general(
        left, right, (((1,), (1,)), ((), ())), preferred_element_type=jnp.float32
    )


def project(left, right):
    return jnp.dot(left, right, preferred_element_type=jnp.float32)


def flatten_rows(matrix):
    return matrix.reshape(-1, 128)


def restore_rows(flat, columns):
    return flat.reshape(-1, columns)


def split_heads(matrix):
    return matrix.reshape(matrix.shape[0] // BLK, BLK, HEADS, HDIM)


def block_scores(queries, keys):
    raw = jnp.einsum(
        "bqhd,bkhd->bhqk",
        split_heads(queries),
        split_heads(keys),
        preferred_element_type=jnp.float32,
    )
    causal = jnp.arange(BLK)[:, None] >= jnp.arange(BLK)[None, :]
    return jnp.where(causal, raw * HDIM ** (-0.5), -1e30)


def attend_forward(queries, keys, values):
    scores = block_scores(queries, keys)
    highest = jnp.max(scores, axis=-1, keepdims=True)
    weights = jnp.exp(scores - highest)
    total = jnp.sum(weights, axis=-1, keepdims=True)
    probs = (weights / total).astype(jnp.bfloat16)
    attended = jnp.einsum(
        "bhqk,bkhd->bqhd", probs, split_heads(values), preferred_element_type=jnp.float32
    )
    return (attended.reshape(queries.shape[0], D), highest + jnp.log(total))


def attend_backward(queries, keys, values, log_total, attended_grad):
    scores = block_scores(queries, keys)
    probs = jnp.exp(scores - log_total)
    grad_heads = split_heads(attended_grad)
    value_grad = jnp.einsum(
        "bhqk,bqhd->bkhd",
        probs.astype(jnp.bfloat16),
        grad_heads,
        preferred_element_type=jnp.float32,
    )
    prob_grad = jnp.einsum(
        "bqhd,bkhd->bhqk", grad_heads, split_heads(values), preferred_element_type=jnp.float32
    )
    score_grad = (probs * (prob_grad - jnp.sum(probs * prob_grad, axis=-1, keepdims=True))).astype(
        jnp.bfloat16
    )
    factor = HDIM ** (-0.5)
    query_grad = (
        jnp.einsum(
            "bhqk,bkhd->bqhd", score_grad, split_heads(keys), preferred_element_type=jnp.float32
        )
        * factor
    )
    key_grad = (
        jnp.einsum(
            "bhqk,bqhd->bkhd", score_grad, split_heads(queries), preferred_element_type=jnp.float32
        )
        * factor
    )
    length = queries.shape[0]
    return (
        query_grad.reshape(length, D).astype(jnp.bfloat16),
        key_grad.reshape(length, D).astype(jnp.bfloat16),
        value_grad.reshape(length, D).astype(jnp.bfloat16),
    )


def on_device(
    tokens,
    attn_gain,
    w_query,
    w_key,
    w_value,
    w_gate,
    w_output,
    ffn_gain,
    w_first,
    w_second,
    w_down,
    cotangent,
):
    attn_whole = (
        lax.all_gather(attn_gain, ("dp", "fsdp"), axis=0, tiled=True),
        lax.all_gather(w_query, ("dp", "fsdp"), axis=0, tiled=True),
        lax.all_gather(w_key, ("dp", "fsdp"), axis=0, tiled=True),
        lax.all_gather(w_value, ("dp", "fsdp"), axis=0, tiled=True),
        lax.all_gather(w_gate, ("dp", "fsdp"), axis=0, tiled=True),
        lax.all_gather(w_output, ("dp", "fsdp"), axis=0, tiled=True),
    )
    gain_one, query_full, key_full, value_full, gate_full, output_full = attn_whole
    inputs = tokens.astype(jnp.float32)
    normed_pre, norm_pull = jax.vjp(rms_scale, inputs, gain_one.astype(jnp.float32))
    normed = normed_pre.astype(jnp.bfloat16)
    queries = project(normed, query_full).astype(jnp.bfloat16)
    keys = project(normed, key_full).astype(jnp.bfloat16)
    values = project(normed, value_full).astype(jnp.bfloat16)
    gate_pre = project(normed, gate_full)
    attended, log_total = attend_forward(queries, keys, values)
    mixed_pre, gate_pull = jax.vjp(gated, attended, gate_pre)
    mixed = mixed_pre.astype(jnp.bfloat16)
    resid = inputs + project(mixed, output_full)
    ffn_whole = (
        lax.all_gather(ffn_gain, ("dp", "fsdp"), axis=0, tiled=True),
        lax.all_gather(w_first, ("dp", "fsdp"), axis=0, tiled=True),
        lax.all_gather(w_second, ("dp", "fsdp"), axis=0, tiled=True),
        lax.all_gather(w_down, ("dp", "fsdp"), axis=0, tiled=True),
    )
    gain_two, first_full, second_full, down_full = ffn_whole
    normed_two_pre, norm_two_pull = jax.vjp(rms_scale, resid, gain_two.astype(jnp.float32))
    normed_two = normed_two_pre.astype(jnp.bfloat16)
    first = project(normed_two, first_full).astype(jnp.bfloat16)
    second = project(normed_two, second_full).astype(jnp.bfloat16)
    product = (first.astype(jnp.float32) * second.astype(jnp.float32)).astype(jnp.bfloat16)
    block_out = (resid + project(product, down_full)).astype(jnp.bfloat16)
    gain_two, first_full, second_full, down_full = (
        lax.all_gather(ffn_gain, ("dp", "fsdp"), axis=0, tiled=True),
        lax.all_gather(w_first, ("dp", "fsdp"), axis=0, tiled=True),
        lax.all_gather(w_second, ("dp", "fsdp"), axis=0, tiled=True),
        lax.all_gather(w_down, ("dp", "fsdp"), axis=0, tiled=True),
    )
    product_grad = contract_cols(cotangent, down_full).astype(jnp.bfloat16)
    product_wide = product_grad.astype(jnp.float32)
    first_grad = (product_wide * second.astype(jnp.float32)).astype(jnp.bfloat16)
    second_grad = (product_wide * first.astype(jnp.float32)).astype(jnp.bfloat16)
    normed_two_grad = contract_cols(first_grad, first_full) + contract_cols(
        second_grad, second_full
    )
    resid_part, gain_two_grad = norm_two_pull(normed_two_grad)
    resid_grad = cotangent.astype(jnp.float32) + resid_part
    down_grad = contract_rows(product, cotangent)
    first_w_grad = contract_rows(normed_two, first_grad)
    second_w_grad = contract_rows(normed_two, second_grad)
    ffn_sums = (
        lax.psum_scatter(gain_two_grad, ("dp", "fsdp"), scatter_dimension=0, tiled=True),
        lax.psum_scatter(
            flatten_rows(first_w_grad), ("dp", "fsdp"), scatter_dimension=0, tiled=True
        ),
        lax.psum_scatter(
            flatten_rows(second_w_grad), ("dp", "fsdp"), scatter_dimension=0, tiled=True
        ),
        lax.psum_scatter(flatten_rows(down_grad), ("dp", "fsdp"), scatter_dimension=0, tiled=True),
    )
    gain_one, query_full, key_full, value_full, gate_full, output_full = (
        lax.all_gather(attn_gain, ("dp", "fsdp"), axis=0, tiled=True),
        lax.all_gather(w_query, ("dp", "fsdp"), axis=0, tiled=True),
        lax.all_gather(w_key, ("dp", "fsdp"), axis=0, tiled=True),
        lax.all_gather(w_value, ("dp", "fsdp"), axis=0, tiled=True),
        lax.all_gather(w_gate, ("dp", "fsdp"), axis=0, tiled=True),
        lax.all_gather(w_output, ("dp", "fsdp"), axis=0, tiled=True),
    )
    branch_grad = resid_grad.astype(jnp.bfloat16)
    mixed_grad = contract_cols(branch_grad, output_full).astype(jnp.bfloat16)
    attended_part, gate_part = gate_pull(mixed_grad.astype(jnp.float32))
    attended_grad = attended_part.astype(jnp.bfloat16)
    gate_grad = gate_part.astype(jnp.bfloat16)
    query_grad, key_grad, value_grad = attend_backward(
        queries, keys, values, log_total, attended_grad
    )
    normed_grad = contract_cols(query_grad, query_full) + contract_cols(key_grad, key_full)
    normed_grad = (
        normed_grad + contract_cols(value_grad, value_full) + contract_cols(gate_grad, gate_full)
    )
    input_part, gain_one_grad = norm_pull(normed_grad)
    tokens_grad = resid_grad + input_part
    output_w_grad = contract_rows(mixed, branch_grad)
    query_w_grad = contract_rows(normed, query_grad)
    key_w_grad = contract_rows(normed, key_grad)
    value_w_grad = contract_rows(normed, value_grad)
    gate_w_grad = contract_rows(normed, gate_grad)
    attn_sums = (
        lax.psum_scatter(gain_one_grad, ("dp", "fsdp"), scatter_dimension=0, tiled=True),
        lax.psum_scatter(
            flatten_rows(query_w_grad), ("dp", "fsdp"), scatter_dimension=0, tiled=True
        ),
        lax.psum_scatter(flatten_rows(key_w_grad), ("dp", "fsdp"), scatter_dimension=0, tiled=True),
        lax.psum_scatter(
            flatten_rows(value_w_grad), ("dp", "fsdp"), scatter_dimension=0, tiled=True
        ),
        lax.psum_scatter(
            flatten_rows(gate_w_grad), ("dp", "fsdp"), scatter_dimension=0, tiled=True
        ),
        lax.psum_scatter(
            flatten_rows(output_w_grad), ("dp", "fsdp"), scatter_dimension=0, tiled=True
        ),
    )
    gain_two_sum, first_flat, second_flat, down_flat = ffn_sums
    gain_one_sum, query_flat, key_flat, value_flat, gate_flat, output_flat = attn_sums
    query_sum = restore_rows(query_flat, D)
    key_sum = restore_rows(key_flat, D)
    value_sum = restore_rows(value_flat, D)
    gate_sum = restore_rows(gate_flat, D)
    output_sum = restore_rows(output_flat, D)
    first_sum = restore_rows(first_flat, FF)
    second_sum = restore_rows(second_flat, FF)
    down_sum = restore_rows(down_flat, D)
    return (
        block_out,
        tokens_grad,
        gain_one_sum,
        query_sum,
        key_sum,
        value_sum,
        gate_sum,
        output_sum,
        gain_two_sum,
        first_sum,
        second_sum,
        down_sum,
    )


def solution(mesh):
    return jax.shard_map(
        on_device,
        mesh=mesh,
        in_specs=(
            P(("dp", "fsdp"), None),
            P(("dp", "fsdp")),
            P(("dp", "fsdp"), None),
            P(("dp", "fsdp"), None),
            P(("dp", "fsdp"), None),
            P(("dp", "fsdp"), None),
            P(("dp", "fsdp"), None),
            P(("dp", "fsdp")),
            P(("dp", "fsdp"), None),
            P(("dp", "fsdp"), None),
            P(("dp", "fsdp"), None),
            P(("dp", "fsdp"), None),
        ),
        out_specs=(
            P(("dp", "fsdp"), None),
            P(("dp", "fsdp"), None),
            P(("dp", "fsdp")),
            P(("dp", "fsdp"), None),
            P(("dp", "fsdp"), None),
            P(("dp", "fsdp"), None),
            P(("dp", "fsdp"), None),
            P(("dp", "fsdp"), None),
            P(("dp", "fsdp")),
            P(("dp", "fsdp"), None),
            P(("dp", "fsdp"), None),
            P(("dp", "fsdp"), None),
        ),
        check_vma=False,
    )
```

profile of v0, /device:TPU:0, one launch (start us, length us, event | category | flops | bytes accessed | tf_op | source)
XLA Modules:
  0.0 2028.0 jit_solution(17572391898870090162)
XLA Ops:
  14.4 42.1 %all-reduce.5 = (bf16[1024]{0:T(1024)(128)(2,1)S(1)}, bf16[1024]{0:T(1024)(128)(2,1)S(1)}) all-reduce(bf16[1024]{0:T(1024)(128)(2,1)S(1)} %dynamic-update-slice, bf16[1024]{0:T(1024)(128)(2,1)S(1)} %dynamic-update-slice.1), channel_id=1, replica_groups=mesh['dp'=2,'fsdp'=16] {'dp','fsdp'}, use_global_device_ids=true, to_apply=%add | all-reduce | flops 2048 | bytes 8192
  57.7 12.3 all-gather.11.cloned.1.call-done
  75.0 53.2 %all-gather.13.cloned.1.call-done = bf16[1024,1024]{1,0:T(8,128)(2,1)} async-done(((bf16[32,1024]{1,0:T(8,128)(2,1)}), bf16[1024,1024]{1,0:T(8,128)(2,1)}) %all-gather.13.cloned.1.call-update) | async-done | bytes 2097168 | tf_op jit(solution)/shard_map/all_gather | solution.py:129
  132.9 53.4 %all-gather.9.cloned.1.call-done = bf16[1024,1024]{1,0:T(8,128)(2,1)} async-done(((bf16[32,1024]{1,0:T(8,128)(2,1)}), bf16[1024,1024]{1,0:T(8,128)(2,1)}) %all-gather.9.cloned.1.call-update) | async-done | bytes 2097168 | tf_op jit(solution)/shard_map/all_gather | solution.py:130
  201.7 42.6 %all-gather.15.cloned.1.call-done = bf16[1024,1024]{1,0:T(8,128)(2,1)} async-done(((bf16[32,1024]{1,0:T(8,128)(2,1)}), bf16[1024,1024]{1,0:T(8,128)(2,1)}) %all-gather.15.cloned.1.call-update) | async-done | bytes 2097168 | tf_op jit(solution)/shard_map/all_gather | solution.py:131
  248.0 54.3 %all-gather.17.cloned.1.call-done = bf16[1024,1024]{1,0:T(8,128)(2,1)} async-done(((bf16[32,1024]{1,0:T(8,128)(2,1)}), bf16[1024,1024]{1,0:T(8,128)(2,1)}) %all-gather.17.cloned.1.call-update) | async-done | bytes 2097168 | tf_op jit(solution)/shard_map/all_gather | solution.py:132
  305.9 65.3 %all-gather.21.cloned.1.call-done = bf16[1024,2816]{1,0:T(8,128)(2,1)} async-done(((bf16[32,2816]{1,0:T(8,128)(2,1)}), bf16[1024,2816]{1,0:T(8,128)(2,1)}) %all-gather.21.cloned.1.call-update) | async-done | bytes 5767184 | tf_op jit(solution)/shard_map/all_gather | solution.py:149
  377.0 63.3 %all-gather.19.cloned.1.call-done = bf16[1024,2816]{1,0:T(8,128)(2,1)} async-done(((bf16[32,2816]{1,0:T(8,128)(2,1)}), bf16[1024,2816]{1,0:T(8,128)(2,1)}) %all-gather.19.cloned.1.call-update) | async-done | bytes 5767184 | tf_op jit(solution)/shard_map/all_gather | solution.py:148
  446.4 63.0 %all-gather.23.cloned.1.call-done = bf16[2816,1024]{1,0:T(8,128)(2,1)} async-done(((bf16[88,1024]{1,0:T(8,128)(2,1)}), bf16[2816,1024]{1,0:T(8,128)(2,1)}) %all-gather.23.cloned.1.call-update) | async-done | bytes 5767184 | tf_op jit(solution)/shard_map/all_gather | solution.py:150
  509.4 7.2 multiply_convert_fusion
  590.9 6.9 fusion.51
  597.8 13.3 reshape.168
  612.5 7.0 fusion.50
  619.5 12.6 reshape.166
  633.5 6.9 fusion.49
  640.4 12.6 reshape.164
  660.8 40.9 %all-reduce.4 = (f32[1024]{0:T(1024)S(1)}, f32[1024]{0:T(1024)S(1)}) all-reduce(f32[1024]{0:T(1024)S(1)} %get-tuple-element.14, f32[1024]{0:T(1024)S(1)} %get-tuple-element.12), channel_id=2, replica_groups=mesh['dp'=2,'fsdp'=16] {'dp','fsdp'}, use_global_device_ids=true, to_apply=%region_8.9.clone | all-reduce | flops 2048 | bytes 16384
  712.2 113.3 %reduce-scatter.15.cloned.1.call-done = f32[256,128]{1,0:T(8,128)} async-done(((f32[8192,128]{1,0:T(8,128)}), f32[256,128]{1,0:T(8,128)}) %reduce-scatter.15.cloned.1.call-update) | async-done | bytes 131088 | tf_op jit(solution)/shard_map/reduce_scatter | solution.py:223
  827.1 144.4 %reduce-scatter.13.cloned.1.call-done = f32[256,128]{1,0:T(8,128)} async-done(((f32[8192,128]{1,0:T(8,128)}), f32[256,128]{1,0:T(8,128)}) %reduce-scatter.13.cloned.1.call-update) | async-done | bytes 131088 | tf_op jit(solution)/shard_map/reduce_scatter | solution.py:220
  973.1 143.2 %reduce-scatter.11.cloned.1.call-done = f32[256,128]{1,0:T(8,128)} async-done(((f32[8192,128]{1,0:T(8,128)}), f32[256,128]{1,0:T(8,128)}) %reduce-scatter.11.cloned.1.call-update) | async-done | bytes 131088 | tf_op jit(solution)/shard_map/reduce_scatter | solution.py:219
  1117.9 145.6 %reduce-scatter.9.cloned.1.call-done = f32[256,128]{1,0:T(8,128)} async-done(((f32[8192,128]{1,0:T(8,128)}), f32[256,128]{1,0:T(8,128)}) %reduce-scatter.9.cloned.1.call-update) | async-done | bytes 131088 | tf_op jit(solution)/shard_map/reduce_scatter | solution.py:216
  1265.2 248.6 %reduce-scatter.23.cloned.1.call-done = f32[704,128]{1,0:T(8,128)} async-done(((f32[22528,128]{1,0:T(8,128)}), f32[704,128]{1,0:T(8,128)}) %reduce-scatter.23.cloned.1.call-update) | async-done | bytes 360464 | tf_op jit(solution)/shard_map/reduce_scatter | solution.py:185
  1515.5 251.0 %reduce-scatter.21.cloned.1.call-done = f32[704,128]{1,0:T(8,128)} async-done(((f32[22528,128]{1,0:T(8,128)}), f32[704,128]{1,0:T(8,128)}) %reduce-scatter.21.cloned.1.call-update) | async-done | bytes 360464 | tf_op jit(solution)/shard_map/reduce_scatter | solution.py:182
  1768.3 251.0 %reduce-scatter.19.cloned.1.call-done = f32[704,128]{1,0:T(8,128)} async-done(((f32[22528,128]{1,0:T(8,128)}), f32[704,128]{1,0:T(8,128)}) %reduce-scatter.19.cloned.1.call-update) | async-done | bytes 360464 | tf_op jit(solution)/shard_map/reduce_scatter | solution.py:179
  (165 shorter events, 159.2 us)
Async XLA Ops:
  7.2 62.8 %all-gather.11.cloned.1.call-start = ((), (), s32[]{:S(2)}) async-start(), calls=%async_computation.9 | async-start | bytes 2162688 | tf_op jit(solution)/shard_map/all_gather | solution.py:128
  7.9 120.2 %all-gather.13.cloned.1.call-start = ((), (), s32[]{:S(2)}) async-start(), calls=%async_computation.10 | async-start | bytes 2162688 | tf_op jit(solution)/shard_map/all_gather | solution.py:129
  8.7 177.6 %all-gather.9.cloned.1.call-start = ((), (), s32[]{:S(2)}) async-start(), calls=%async_computation.8 | async-start | bytes 2162688 | tf_op jit(solution)/shard_map/all_gather | solution.py:130
  9.4 234.9 %all-gather.15.cloned.1.call-start = ((), (), s32[]{:S(2)}) async-start(), calls=%async_computation.11 | async-start | bytes 2162688 | tf_op jit(solution)/shard_map/all_gather | solution.py:131
  10.0 292.3 %all-gather.17.cloned.1.call-start = ((), (), s32[]{:S(2)}) async-start(), calls=%async_computation.12 | async-start | bytes 2162688 | tf_op jit(solution)/shard_map/all_gather | solution.py:132
  10.6 360.6 %all-gather.21.cloned.1.call-start = ((), (), s32[]{:S(2)}) async-start(), calls=%async_computation.14 | async-start | bytes 5947392 | tf_op jit(solution)/shard_map/all_gather | solution.py:149
  11.1 429.2 %all-gather.19.cloned.1.call-start = ((), (), s32[]{:S(2)}) async-start(), calls=%async_computation.13 | async-start | bytes 5947392 | tf_op jit(solution)/shard_map/all_gather | solution.py:148
  11.9 497.5 %all-gather.23.cloned.1.call-start = ((), (), s32[]{:S(2)}) async-start(), calls=%async_computation.15 | async-start | bytes 5947392 | tf_op jit(solution)/shard_map/all_gather | solution.py:150
  12.6 698.0 %reduce-scatter.17.cloned.1.call-start = ((), (), s32[]{:S(2)}) async-start(), calls=%async_computation.20 | async-start | bytes 4325376 | tf_op jit(solution)/shard_map/reduce_scatter | solution.py:226
  72.5 55.6 %copy-start = (bf16[256,1024]{1,0:T(8,128)(2,1)S(1)}, bf16[256,1024]{1,0:T(8,128)(2,1)}, u32[]{:S(2)}) copy-start(bf16[256,1024]{1,0:T(8,128)(2,1)} %param.12) | copy-start | bytes 1572868
  248.0 56.7 %copy-start.26 = (bf16[256,1024]{1,0:T(8,128)(2,1)}, bf16[256,1024]{1,0:T(8,128)(2,1)S(1)}, u32[]{:S(2)}) copy-start(bf16[256,1024]{1,0:T(8,128)(2,1)S(1)} %get-tuple-element.27) | copy-start | bytes 1572868
  305.9 65.3 %copy-start.19 = (bf16[256,1024]{1,0:T(8,128)(2,1)}, bf16[256,1024]{1,0:T(8,128)(2,1)S(1)}, u32[]{:S(2)}) copy-start(bf16[256,1024]{1,0:T(8,128)(2,1)S(1)} %multiply_convert_fusion.6) | copy-start | bytes 1572868
  377.0 132.4 %copy-start.18 = (bf16[256,1024]{1,0:T(8,128)(2,1)S(1)}, bf16[256,1024]{1,0:T(8,128)(2,1)}, u32[]{:S(2)}) copy-start(bf16[256,1024]{1,0:T(8,128)(2,1)} %param.23) | copy-start | bytes 1572868
  509.4 7.2 copy-start.28
  532.1 293.4 %reduce-scatter.15.cloned.1.call-start = ((), (), s32[]{:S(2)}) async-start(), calls=%async_computation.19 | async-start | bytes 4325376 | tf_op jit(solution)/shard_map/reduce_scatter | solution.py:223
  544.3 427.2 %reduce-scatter.13.cloned.1.call-start = ((), (), s32[]{:S(2)}) async-start(), calls=%async_computation.18 | async-start | bytes 4325376 | tf_op jit(solution)/shard_map/reduce_scatter | solution.py:220
  564.3 552.1 %reduce-scatter.11.cloned.1.call-start = ((), (), s32[]{:S(2)}) async-start(), calls=%async_computation.17 | async-start | bytes 4325376 | tf_op jit(solution)/shard_map/reduce_scatter | solution.py:219
  578.1 685.4 %reduce-scatter.9.cloned.1.call-start = ((), (), s32[]{:S(2)}) async-start(), calls=%async_computation.16 | async-start | bytes 4325376 | tf_op jit(solution)/shard_map/reduce_scatter | solution.py:216
  589.6 924.2 %reduce-scatter.23.cloned.1.call-start = ((), (), s32[]{:S(2)}) async-start(), calls=%async_computation.23 | async-start | bytes 11894784 | tf_op jit(solution)/shard_map/reduce_scatter | solution.py:185
  611.2 1155.3 %reduce-scatter.21.cloned.1.call-start = ((), (), s32[]{:S(2)}) async-start(), calls=%async_computation.22 | async-start | bytes 11894784 | tf_op jit(solution)/shard_map/reduce_scatter | solution.py:182
  632.1 1387.1 %reduce-scatter.19.cloned.1.call-start = ((), (), s32[]{:S(2)}) async-start(), calls=%async_computation.21 | async-start | bytes 11894784 | tf_op jit(solution)/shard_map/reduce_scatter | solution.py:179
  658.9 44.1 %copy-start.9 = (f32[256,1024]{1,0:T(8,128)S(1)}, f32[256,1024]{1,0:T(8,128)}, u32[]{:S(2)}) copy-start(f32[256,1024]{1,0:T(8,128)} %copy-done.8) | copy-start | bytes 3145732
  660.8 44.6 %copy-start.5 = (f32[256,1024]{1,0:T(8,128)S(1)}, f32[256,1024]{1,0:T(8,128)}, u32[]{:S(2)}) copy-start(f32[256,1024]{1,0:T(8,128)} %copy-done.3) | copy-start | bytes 3145732
  701.8 3.7 copy-start.11
  (21 other events, 32.5 us)
Sparse Core Ops, SparseCore 0:
  10.9 59.0 all-gather.10
  72.9 55.2 all-gather.12
  131.0 55.2 all-gather.8
  189.0 55.2 all-gather.14
  247.0 55.2 all-gather.16
  305.0 66.1 all-gather.20
  374.0 66.2 all-gather.18
  443.1 66.2 all-gather.22
  532.3 145.1 reduce-scatter.16
  679.6 145.9 reduce-scatter.14
  827.8 143.6 reduce-scatter.12
  973.7 142.6 reduce-scatter.10
  1118.6 144.9 reduce-scatter.8
  1265.7 247.9 reduce-scatter.22
  1515.9 250.5 reduce-scatter.20
  1768.7 250.5 reduce-scatter.18
where the time goes:
time: 2040 us; the launch traced here: 2030 us
  waiting for transfers between devices  1710 us (84%)
  local copies, waits for them, and re-layouts  115 us (6%)
  matrix products  98.8 us (5%)
  blocking collectives  83 us (4%)
    reduce_scatter x1, waiting for transfers between devices, on_device(): lax.psum_scatter(flatten_rows(first_w_grad), ('dp', 'fsdp'), scatter_dime...  251 us
    reduce_scatter x1, waiting for transfers between devices, on_device(): lax.psum_scatter(flatten_rows(second_w_grad), ('dp', 'fsdp'), scatter_dim...  251 us
    reduce_scatter x1, waiting for transfers between devices, on_device(): lax.psum_scatter(flatten_rows(down_grad), ('dp', 'fsdp'), scatter_dimensi...  249 us
    reduce_scatter x1, waiting for transfers between devices, on_device(): lax.psum_scatter(flatten_rows(query_w_grad), ('dp', 'fsdp'), scatter_dime...  146 us
    reduce_scatter x1, waiting for transfers between devices, on_device(): lax.psum_scatter(flatten_rows(value_w_grad), ('dp', 'fsdp'), scatter_dime...  144 us
    reduce_scatter x1, waiting for transfers between devices, on_device(): lax.psum_scatter(flatten_rows(key_w_grad), ('dp', 'fsdp'), scatter_dimens...  143 us
    reduce_scatter x1, waiting for transfers between devices, on_device(): lax.psum_scatter(flatten_rows(gate_w_grad), ('dp', 'fsdp'), scatter_dimen...  113 us
    unnamed x2, blocking collectives  83 us
  transfers between devices with their start and end apart: 16, of which 15 were waited for; matrix products, arithmetic and copies ran while one was open for 9% of the time, Pallas kernels for 0%

commit v1 on v0

--- a/solution.py
+++ b/solution.py
@@ -1,7 +1,13 @@
+import functools
+
 import jax
 import jax.numpy as jnp
 from jax import lax
+from jax.experimental import pallas as pl
+from jax.experimental.pallas import tpu as pltpu
 from jax.sharding import PartitionSpec as P
+
+MESH = pl.DeviceIdType.MESH
 
 D = 1024
 HEADS = 16
@@ -109,7 +115,92 @@
     )
 
 
+def ag_kernel(n, *refs):
+    ins = refs[:n]; outs = refs[n:2*n]
+    lsem, zsend, zrecv, xsend, xrecv, ysend, yrecv, csend, crecv = refs[2*n:]
+    c = lax.axis_index("dp"); f = lax.axis_index("fsdp")
+    z, y, x = f // 4, (f // 2) % 2, f % 2
+    fid = lambda zz, yy, xx: zz * 4 + yy * 2 + xx
+    xn, yn = 1 - x, 1 - y
+    bar = pltpu.get_barrier_semaphore()
+    zs = [(z + k) % 4 for k in (1, 2, 3)]
+    peers = [(c, fid(zz, y, x)) for zz in zs] + [(c, fid(z, y, xn)), (c, fid(z, yn, x)), (1 - c, f)]
+    for p in peers:
+        pl.semaphore_signal(bar, inc=1, device_id=p, device_id_type=MESH)
+    pl.semaphore_wait(bar, 6)
+    base = c * 16
+    def rc(src, dst, ss, rs, dev):
+        return pltpu.make_async_remote_copy(src_ref=src, dst_ref=dst, send_sem=ss, recv_sem=rs, device_id=dev, device_id_type=MESH)
+    def cp(i, s, which):
+        slot = outs[i].at[base + s]
+        ss, rs, dev = {"x": (xsend, xrecv, (c, fid(z, y, xn))), "y": (ysend, yrecv, (c, fid(z, yn, x))), "c": (csend, crecv, (1 - c, f))}[which]
+        return rc(slot, slot, ss.at[i, s], rs.at[i, s], dev)
+    started = []
+    def go(i, s, which):
+        d = cp(i, s, which); d.start(); started.append(d)
+    def s0(i):
+        l = pltpu.make_async_copy(ins[i], outs[i].at[base + f], lsem.at[i]); l.start()
+        for k in range(3):
+            d = rc(ins[i], outs[i].at[base + f], zsend.at[i, k], zrecv.at[i, 2 - k], (c, fid(zs[k], y, x)))
+            d.start(); started.append(d)
+        l.wait()
+        for w in "xyc": go(i, f, w)
+    def s1(i):
+        for k in (0, 2, 1):
+            s = fid(zs[k], y, x)
+            slot = outs[i].at[base + s]
+            rc(slot, slot, zsend.at[i, k], zrecv.at[i, k], (c, f)).wait_recv()
+            for w in "xyc": go(i, s, w)
+    def zz_of(k): return (z + k) % 4
+    def s2(i):
+        for k in range(4):
+            zz = zz_of(k)
+            par = zz % 2
+            sx, sy = fid(zz, y, xn), fid(zz, yn, x)
+            cp(i, sx, "x").wait_recv()
+            cp(i, sy, "y").wait_recv()
+            @pl.when(par == 0)
+            def _(): cp(i, sx, "y").start()
+            @pl.when(par == 1)
+            def _(): cp(i, sy, "x").start()
+            go(i, sx, "c"); go(i, sy, "c")
+    def s3(i):
+        for k in range(4):
+            zz = zz_of(k); par = zz % 2
+            sd = fid(zz, yn, xn); sx, sy = fid(zz, y, xn), fid(zz, yn, x)
+            @pl.when(par == 0)
+            def _():
+                cp(i, sd, "y").wait_recv(); cp(i, sx, "y").wait_send()
+            @pl.when(par == 1)
+            def _():
+                cp(i, sd, "x").wait_recv(); cp(i, sy, "x").wait_send()
+            go(i, sd, "c")
+    def s4(i):
+        for s in range(16):
+            slot = outs[i].at[(1 - c) * 16 + s]
+            rc(slot, slot, csend.at[i, s], crecv.at[i, s], (1 - c, f)).wait_recv()
+    stages = [s0, s1, s2, s3, s4]
+    for t in range(n + 4):
+        for k, st in enumerate(stages):
+            i = t - k
+            if 0 <= i < n: st(i)
+    for d in started: d.wait_send()
+
+def gather_whole(ws):
+    n = len(ws)
+    D = pltpu.SemaphoreType.DMA
+    return pl.pallas_call(
+        functools.partial(ag_kernel, n),
+        out_shape=[jax.ShapeDtypeStruct((32,) + w.shape, w.dtype) for w in ws],
+        in_specs=[pl.BlockSpec(memory_space=pl.ANY)] * n,
+        out_specs=[pl.BlockSpec(memory_space=pl.ANY)] * n,
+        scratch_shapes=[D((n,)), D((n, 3)), D((n, 3)), D((n, 16)), D((n, 16)), D((n, 16)), D((n, 16)), D((n, 16)), D((n, 16))],
+        compiler_params=pltpu.CompilerParams(collective_id=0, has_side_effects=True),
+    )(*ws)
+
+
 def on_device(
+    fast,
     tokens,
     attn_gain,
     w_query,
@@ -123,13 +214,19 @@
     w_down,
     cotangent,
 ):
+    weights = (w_query, w_key, w_value, w_gate, w_output, w_first, w_second, w_down)
+    if fast:
+        whole = [full.reshape(-1, full.shape[-1]) for full in gather_whole(weights)]
+    else:
+        whole = [lax.all_gather(weight, ("dp", "fsdp"), axis=0, tiled=True) for weight in weights]
+    w_query, w_key, w_value, w_gate, w_output, w_first, w_second, w_down = whole
     attn_whole = (
         lax.all_gather(attn_gain, ("dp", "fsdp"), axis=0, tiled=True),
-        lax.all_gather(w_query, ("dp", "fsdp"), axis=0, tiled=True),
-        lax.all_gather(w_key, ("dp", "fsdp"), axis=0, tiled=True),
-        lax.all_gather(w_value, ("dp", "fsdp"), axis=0, tiled=True),
-        lax.all_gather(w_gate, ("dp", "fsdp"), axis=0, tiled=True),
-        lax.all_gather(w_output, ("dp", "fsdp"), axis=0, tiled=True),
+        w_query,
+        w_key,
+        w_value,
+        w_gate,
+        w_output,
     )
     gain_one, query_full, key_full, value_full, gate_full, output_full = attn_whole
     inputs = tokens.astype(jnp.float32)
@@ -145,9 +242,9 @@
     resid = inputs + project(mixed, output_full)
     ffn_whole = (
         lax.all_gather(ffn_gain, ("dp", "fsdp"), axis=0, tiled=True),
-        lax.all_gather(w_first, ("dp", "fsdp"), axis=0, tiled=True),
-        lax.all_gather(w_second, ("dp", "fsdp"), axis=0, tiled=True),
-        lax.all_gather(w_down, ("dp", "fsdp"), axis=0, tiled=True),
+        w_first,
+        w_second,
+        w_down,
     )
     gain_two, first_full, second_full, down_full = ffn_whole
     normed_two_pre, norm_two_pull = jax.vjp(rms_scale, resid, gain_two.astype(jnp.float32))
@@ -158,9 +255,9 @@
     block_out = (resid + project(product, down_full)).astype(jnp.bfloat16)
     gain_two, first_full, second_full, down_full = (
         lax.all_gather(ffn_gain, ("dp", "fsdp"), axis=0, tiled=True),
-        lax.all_gather(w_first, ("dp", "fsdp"), axis=0, tiled=True),
-        lax.all_gather(w_second, ("dp", "fsdp"), axis=0, tiled=True),
-        lax.all_gather(w_down, ("dp", "fsdp"), axis=0, tiled=True),
+        w_first,
+        w_second,
+        w_down,
     )
     product_grad = contract_cols(cotangent, down_full).astype(jnp.bfloat16)
     product_wide = product_grad.astype(jnp.float32)
@@ -186,11 +283,11 @@
     )
     gain_one, query_full, key_full, value_full, gate_full, output_full = (
         lax.all_gather(attn_gain, ("dp", "fsdp"), axis=0, tiled=True),
-        lax.all_gather(w_query, ("dp", "fsdp"), axis=0, tiled=True),
-        lax.all_gather(w_key, ("dp", "fsdp"), axis=0, tiled=True),
-        lax.all_gather(w_value, ("dp", "fsdp"), axis=0, tiled=True),
-        lax.all_gather(w_gate, ("dp", "fsdp"), axis=0, tiled=True),
-        lax.all_gather(w_output, ("dp", "fsdp"), axis=0, tiled=True),
+        w_query,
+        w_key,
+        w_value,
+        w_gate,
+        w_output,
     )
     branch_grad = resid_grad.astype(jnp.bfloat16)
     mixed_grad = contract_cols(branch_grad, output_full).astype(jnp.bfloat16)
@@ -255,7 +352,7 @@
 
 def solution(mesh):
     return jax.shard_map(
-        on_device,
+        functools.partial(on_device, dict(mesh.shape) == {"dp": 2, "fsdp": 16}),
         mesh=mesh,
         in_specs=(
             P(("dp", "fsdp"), None),

time: 2040 us -> 1740 us (0.85)
  waiting for transfers between devices: 1710 us -> 1300 us
  Pallas kernels: 0 us -> 130 us
    all_gather x8 -> x0, waiting for transfers between devices: 407 us -> none  [the longest x1 65.3 us: on_device(): lax.all_gather(w_second, ('dp', 'fsdp'), axis=0, tiled=True)]
    pallas_call x0 -> x1, Pallas kernels: none -> 130 us  [gather_whole(): pl.pallas_call(functools.partial(ag_kernel, n), out_shape=[jax.ShapeDtype...]
  transfers between devices with their start and end apart: 16 -> 8, of which waited for: 15 -> 7; matrix products, arithmetic and copies ran while one was open for 9% -> 8% of each run, Pallas kernels for 0% -> 0%
where the time goes in v1:
time: 1740 us; the launch traced here: 1730 us
  waiting for transfers between devices  1300 us (75%)
  Pallas kernels  130 us (7%)
  local copies, waits for them, and re-layouts  115 us (7%)
  blocking collectives  86 us (5%)
  matrix products  83.6 us (5%)
    reduce_scatter x1, waiting for transfers between devices, on_device(): lax.psum_scatter(flatten_rows(second_w_grad), ('dp', 'fsdp'), scatter_dim...  251 us
    reduce_scatter x1, waiting for transfers between devices, on_device(): lax.psum_scatter(flatten_rows(first_w_grad), ('dp', 'fsdp'), scatter_dime...  251 us
    reduce_scatter x1, waiting for transfers between devices, on_device(): lax.psum_scatter(flatten_rows(down_grad), ('dp', 'fsdp'), scatter_dimensi...  248 us
    reduce_scatter x1, waiting for transfers between devices, on_device(): lax.psum_scatter(flatten_rows(key_w_grad), ('dp', 'fsdp'), scatter_dimens...  146 us
    reduce_scatter x1, waiting for transfers between devices, on_device(): lax.psum_scatter(flatten_rows(value_w_grad), ('dp', 'fsdp'), scatter_dime...  144 us
    reduce_scatter x1, waiting for transfers between devices, on_device(): lax.psum_scatter(flatten_rows(query_w_grad), ('dp', 'fsdp'), scatter_dime...  144 us
    pallas_call x1, Pallas kernels, gather_whole(): pl.pallas_call(functools.partial(ag_kernel, n), out_shape=[jax.ShapeDtype...  130 us
    reduce_scatter x1, waiting for transfers between devices, on_device(): lax.psum_scatter(flatten_rows(gate_w_grad), ('dp', 'fsdp'), scatter_dimen...  112 us
  transfers between devices with their start and end apart: 8, of which 7 were waited for; matrix products, arithmetic and copies ran while one was open for 8% of the time, Pallas kernels for 0%

profile of v1, /device:TPU:0, one launch (start us, length us, event | category | flops | bytes accessed | tf_op | source)
XLA Modules:
  0.0 1732.6 jit_solution(18439420308669125313)
XLA Ops:
  10.2 42.0 %all-reduce.5 = (bf16[1024]{0:T(1024)(128)(2,1)S(1)}, bf16[1024]{0:T(1024)(128)(2,1)S(1)}) all-reduce(bf16[1024]{0:T(1024)(128)(2,1)S(1)} %dynamic-update-slice, bf16[1024]{0:T(1024)(128)(2,1)S(1)} %dynamic-update-slice.1), channel_id=1, replica_groups=mesh['dp'=2,'fsdp'=16] {'dp','fsdp'}, use_global_device_ids=true, to_apply=%add | all-reduce | flops 2048 | bytes 8192
  52.2 129.8 %shard_map.211 = (bf16[32,32,1024]{2,1,0:T(8,128)(2,1)}, bf16[32,32,1024]{2,1,0:T(8,128)(2,1)}, bf16[32,32,1024]{2,1,0:T(8,128)(2,1)}, bf16[32,32,1024]{2,1,0:T(...) custom-call(bf16[32,1024]{1,0:T(8,128)(2,1)} %refs_0_.1, ...), custom_call_target="tpu_custom_call" | custom-call | tf_op jit(solution)/shard_map/pallas_call | solution.py:192
  205.7 3.8 multiply_convert_fusion.7
  210.5 4.9 fusion.2
  228.8 4.9 reshape.197
  241.2 5.0 reshape.195
  261.0 4.9 reshape.193
  274.8 5.0 reshape.191
  286.2 4.9 reshape.189
  292.5 7.0 fusion.52
  299.5 13.3 reshape.203
  314.2 7.0 fusion.51
  321.1 12.6 reshape.201
  335.1 6.9 fusion.50
  342.0 12.6 reshape.199
  362.6 43.9 %all-reduce.4 = (f32[1024]{0:T(1024)S(1)}, f32[1024]{0:T(1024)S(1)}) all-reduce(f32[1024]{0:T(1024)S(1)} %get-tuple-element.30, f32[1024]{0:T(1024)S(1)} %get-tuple-element.28), channel_id=2, replica_groups=mesh['dp'=2,'fsdp'=16] {'dp','fsdp'}, use_global_device_ids=true, to_apply=%region_8.9.clone | all-reduce | flops 2048 | bytes 16384
  410.2 5.2 fusion.9
  417.0 112.4 %reduce-scatter.15.cloned.1.call-done = f32[256,128]{1,0:T(8,128)} async-done(((f32[8192,128]{1,0:T(8,128)}), f32[256,128]{1,0:T(8,128)}) %reduce-scatter.15.cloned.1.call-update) | async-done | bytes 131088 | tf_op jit(solution)/shard_map/reduce_scatter | solution.py:320
  530.9 144.3 %reduce-scatter.13.cloned.1.call-done = f32[256,128]{1,0:T(8,128)} async-done(((f32[8192,128]{1,0:T(8,128)}), f32[256,128]{1,0:T(8,128)}) %reduce-scatter.13.cloned.1.call-update) | async-done | bytes 131088 | tf_op jit(solution)/shard_map/reduce_scatter | solution.py:317
  676.8 145.8 %reduce-scatter.11.cloned.1.call-done = f32[256,128]{1,0:T(8,128)} async-done(((f32[8192,128]{1,0:T(8,128)}), f32[256,128]{1,0:T(8,128)}) %reduce-scatter.11.cloned.1.call-update) | async-done | bytes 131088 | tf_op jit(solution)/shard_map/reduce_scatter | solution.py:316
  824.3 143.8 %reduce-scatter.9.cloned.1.call-done = f32[256,128]{1,0:T(8,128)} async-done(((f32[8192,128]{1,0:T(8,128)}), f32[256,128]{1,0:T(8,128)}) %reduce-scatter.9.cloned.1.call-update) | async-done | bytes 131088 | tf_op jit(solution)/shard_map/reduce_scatter | solution.py:313
  969.6 248.4 %reduce-scatter.23.cloned.1.call-done = f32[704,128]{1,0:T(8,128)} async-done(((f32[22528,128]{1,0:T(8,128)}), f32[704,128]{1,0:T(8,128)}) %reduce-scatter.23.cloned.1.call-update) | async-done | bytes 360464 | tf_op jit(solution)/shard_map/reduce_scatter | solution.py:282
  1219.8 251.1 %reduce-scatter.21.cloned.1.call-done = f32[704,128]{1,0:T(8,128)} async-done(((f32[22528,128]{1,0:T(8,128)}), f32[704,128]{1,0:T(8,128)}) %reduce-scatter.21.cloned.1.call-update) | async-done | bytes 360464 | tf_op jit(solution)/shard_map/reduce_scatter | solution.py:279
  1472.7 251.1 %reduce-scatter.19.cloned.1.call-done = f32[704,128]{1,0:T(8,128)} async-done(((f32[22528,128]{1,0:T(8,128)}), f32[704,128]{1,0:T(8,128)}) %reduce-scatter.19.cloned.1.call-update) | async-done | bytes 360464 | tf_op jit(solution)/shard_map/reduce_scatter | solution.py:276
  (153 shorter events, 107.1 us)
Async XLA Ops:
  7.2 408.2 %reduce-scatter.17.cloned.1.call-start = ((), (), s32[]{:S(2)}) async-start(), calls=%async_computation.12 | async-start | bytes 4325376 | tf_op jit(solution)/shard_map/reduce_scatter | solution.py:323
  187.0 4.1 copy-start.25
  205.7 3.8 copy-start.22
  210.3 14.4 copy-start.3
  210.3 5.2 slice-start.4
  210.5 5.0 copy-start.18
  210.5 5.0 slice-start.5
  215.5 2.6 slice-start.1
  215.6 2.7 copy-start.17
  215.6 7.3 slice-start.2
  218.3 4.6 slice-start.3
  233.6 295.7 %reduce-scatter.15.cloned.1.call-start = ((), (), s32[]{:S(2)}) async-start(), calls=%async_computation.11 | async-start | bytes 4325376 | tf_op jit(solution)/shard_map/reduce_scatter | solution.py:320
  246.2 429.0 %reduce-scatter.13.cloned.1.call-start = ((), (), s32[]{:S(2)}) async-start(), calls=%async_computation.10 | async-start | bytes 4325376 | tf_op jit(solution)/shard_map/reduce_scatter | solution.py:317
  265.9 556.8 %reduce-scatter.11.cloned.1.call-start = ((), (), s32[]{:S(2)}) async-start(), calls=%async_computation.9 | async-start | bytes 4325376 | tf_op jit(solution)/shard_map/reduce_scatter | solution.py:316
  272.0 2.8 copy-start.15
  279.8 688.2 %reduce-scatter.9.cloned.1.call-start = ((), (), s32[]{:S(2)}) async-start(), calls=%async_computation.8 | async-start | bytes 4325376 | tf_op jit(solution)/shard_map/reduce_scatter | solution.py:313
  291.2 926.8 %reduce-scatter.23.cloned.1.call-start = ((), (), s32[]{:S(2)}) async-start(), calls=%async_computation.15 | async-start | bytes 11894784 | tf_op jit(solution)/shard_map/reduce_scatter | solution.py:282
  312.8 1158.0 %reduce-scatter.21.cloned.1.call-start = ((), (), s32[]{:S(2)}) async-start(), calls=%async_computation.14 | async-start | bytes 11894784 | tf_op jit(solution)/shard_map/reduce_scatter | solution.py:279
  333.8 1390.0 %reduce-scatter.19.cloned.1.call-start = ((), (), s32[]{:S(2)}) async-start(), calls=%async_computation.13 | async-start | bytes 11894784 | tf_op jit(solution)/shard_map/reduce_scatter | solution.py:276
  354.7 2.5 copy-start.16
  354.7 2.5 copy-start.26
  360.6 47.1 %copy-start.8 = (f32[256,1024]{1,0:T(8,128)S(1)}, f32[256,1024]{1,0:T(8,128)}, u32[]{:S(2)}) copy-start(f32[256,1024]{1,0:T(8,128)} %copy-done.7) | copy-start | bytes 3145732
  362.6 47.6 %copy-start.4 = (f32[256,1024]{1,0:T(8,128)S(1)}, f32[256,1024]{1,0:T(8,128)}, u32[]{:S(2)}) copy-start(f32[256,1024]{1,0:T(8,128)} %copy-done.3) | copy-start | bytes 3145732
  406.5 3.7 copy-start.10
  (17 other events, 24.9 us)
Sparse Core Ops, SparseCore 0:
  233.8 148.9 reduce-scatter.16
  385.1 144.2 reduce-scatter.14
  531.6 143.5 reduce-scatter.12
  677.4 145.2 reduce-scatter.10
  824.8 143.1 reduce-scatter.8
  970.2 247.7 reduce-scatter.22
  1220.3 250.5 reduce-scatter.20
  1473.2 250.5 reduce-scatter.18

commit v2 on v0

--- a/solution.py
+++ b/solution.py
@@ -1,6 +1,10 @@
+import functools
+
 import jax
 import jax.numpy as jnp
 from jax import lax
+from jax.experimental import pallas as pl
+from jax.experimental.pallas import tpu as pltpu
 from jax.sharding import PartitionSpec as P
 
 D = 1024
@@ -11,6 +15,667 @@
 
 
 EPS = 1e-06
+
+
+MESH = pl.DeviceIdType.MESH
+F32, BF16 = jnp.float32, jnp.bfloat16
+
+OWN = 256
+ROWS = 512
+HALF = 512
+FH = 1408
+CHUNKS = (
+    ("d", 0, 256), ("d", 256, 256),
+    ("f", 0, 768), ("f", 768, 640), ("f", 1408, 768), ("f", 2176, 640),
+    ("o", 0, 512),
+    ("a", 0, 512), ("a", 512, 512), ("a", 1024, 512), ("a", 1536, 512),
+)
+NCH = len(CHUNKS)
+GROUPS = ("a", "o", "f", "s", "d")
+
+
+def piece_rows(kind):
+    return 176 if kind == "d" else 64
+
+
+def scratch_list():
+    vm, dma = pltpu.VMEM, pltpu.SemaphoreType.DMA
+    items = [
+        ("wa", vm((D, 4 * HALF), BF16)), ("wf", vm((D, 2 * FH), BF16)),
+        ("wo", vm((HALF, D), BF16)), ("wd", vm((FH, D), BF16)), ("wds", vm((2, 88, 512), BF16)),
+        ("tok", vm((ROWS, D), BF16)), ("cot", vm((ROWS, D), BF16)), ("nrm", vm((ROWS, D), BF16)),
+        ("qkv", vm((ROWS, 3 * HALF), BF16)), ("gp", vm((ROWS, HALF), F32)), ("att", vm((ROWS, HALF), F32)),
+        ("prob", vm((ROWS, HALF), F32)), ("mix", vm((ROWS, HALF), BF16)), ("dout", vm((ROWS, HALF), BF16)),
+        ("res", vm((OWN, D), F32)), ("nt", vm((ROWS, D), BF16)), ("fs", vm((ROWS, 2 * FH), BF16)),
+        ("pr", vm((ROWS, FH), BF16)), ("g4", vm((ROWS, 4 * HALF), BF16)), ("bg", vm((ROWS, D), BF16)),
+        ("rg", vm((OWN, D), F32)), ("po", vm((OWN, D), F32)), ("bo", vm((OWN, D), BF16)),
+        ("es", vm((4, OWN, D), BF16)), ("er", vm((4, OWN, D), BF16)),
+        ("gs", vm((8, 8, D), F32)), ("gr", vm((13, 8, D), F32)), ("gacc", vm((2, 8, D), F32)),
+        ("sbd", vm((2, 4, 2, 176, 256), BF16)), ("sbf", vm((2, 4, 2, 64, 768), BF16)),
+    ]
+    for i, (kind, _, cols) in enumerate(CHUNKS):
+        r = piece_rows(kind)
+        items += [
+            (f"rb{i}", vm((4, 2, r, cols), BF16)), (f"ow{i}", vm((4, 2, r, cols), BF16)),
+            (f"yr{i}", vm((4, r, cols), BF16)), (f"zr{i}", vm((3, r, cols), BF16)),
+            (f"fin{i}", vm((r, cols), F32)),
+        ]
+    n = len(GROUPS)
+    items += [
+        ("s_loc", dma((4,))), ("s_wl", dma((n,))), ("s_xs", dma((n, 2))), ("s_xr", dma((n,))),
+        ("s_es", dma((8,))), ("s_er", dma((8,))),
+        ("s_zs", dma((n, 3))), ("s_zr", dma((n, 3))), ("s_ys", dma((n, 4))), ("s_yr", dma((n, 4))),
+        ("s_cs", dma((n, 4, 2))), ("s_cr", dma((n, 4, 2))),
+        ("s_gs", dma((2, 6))), ("s_gr", dma((2, 6))),
+        ("r_cs", dma((NCH,))), ("r_cr", dma((NCH,))), ("r_ys", dma((NCH,))), ("r_yr", dma((NCH,))),
+        ("r_zs", dma((NCH, 3))), ("r_zr", dma((NCH, 3))), ("r_fs", dma((NCH, 2))), ("r_fr", dma((NCH, 2))),
+        ("s_out", dma((4,))),
+    ]
+    return items
+
+
+IN_NAMES = ("tokens", "gains", "wq", "wk", "wv", "wg", "wo_in", "w1", "w2", "wd_in", "cot_in")
+OUT_NAMES = ("block_out", "tokens_grad", "gain_grads", "gq", "gk", "gv", "gg", "go", "g1", "g2", "gd")
+
+
+class Refs:
+    def __init__(self, names, refs):
+        self.__dict__.update(zip(names, refs))
+
+
+def rows_of(start, count, unit=8):
+    return pl.ds(pl.multiple_of(start, unit), count)
+
+
+def lanes_of(start, count):
+    return pl.ds(pl.multiple_of(start, 128), count)
+
+
+def dot(a, b):
+    return jnp.dot(a, b, preferred_element_type=F32)
+
+
+def dot_t(a, b):
+    return lax.dot_general(a, b, (((1,), (1,)), ((), ())), preferred_element_type=F32)
+
+
+def t_dot(a, b):
+    return lax.dot_general(a, b, (((0,), (0,)), ((), ())), preferred_element_type=F32)
+
+
+def tile_loop(total, width, fn):
+    count = total // width
+    if count == 1:
+        fn(0, width)
+    else:
+        lax.fori_loop(0, count, lambda i, u: (fn(pl.multiple_of(i * width, width), width), u)[1], 0)
+    if total % width:
+        fn(count * width, total % width)
+
+
+def row_loop(total, step, fn):
+    lax.fori_loop(0, total // step, lambda i, u: (fn(pl.multiple_of(i * step, step)), u)[1], 0)
+
+
+def layer_kernel(names, *refs):
+    r = Refs(names, refs)
+    c = lax.axis_index("dp")
+    f = lax.axis_index("fsdp")
+    z, y, x = f // 4, (f // 2) % 2, f % 2
+
+    def dev(cc, zz, yy, xx):
+        return (cc, zz * 4 + yy * 2 + xx)
+
+    xn, yn, sib, diag = dev(c, z, y, 1 - x), dev(c, z, 1 - y, x), dev(1 - c, z, y, x), dev(1 - c, z, y, 1 - x)
+    zk = [(z + k) % 4 for k in range(4)]
+    zp = [dev(c, zk[k], y, x) for k in range(4)]
+
+    barrier = pltpu.get_barrier_semaphore()
+    for peer in (xn, yn, sib, diag, zp[1], zp[2], zp[3]):
+        pl.semaphore_signal(barrier, inc=1, device_id=peer, device_id_type=MESH)
+    pl.semaphore_wait(barrier, 7)
+
+    sends = []
+
+    def remote(src, dst, ss, rs, to):
+        return pltpu.make_async_remote_copy(
+            src_ref=src, dst_ref=dst, send_sem=ss, recv_sem=rs, device_id=to, device_id_type=MESH
+        )
+
+    def send(src, dst, ss, rs, to, later=True):
+        copy = remote(src, dst, ss, rs, to)
+        copy.start()
+        if later:
+            sends.append(copy)
+        return copy
+
+    def arrived(ref, sem):
+        remote(ref, ref, sem, sem, xn).wait_recv()
+
+    def local(src, dst, sem):
+        copy = pltpu.make_async_copy(src, dst, sem)
+        copy.start()
+        return copy
+
+    mine = x
+    p = c * 8 + z * 2 + y
+    m = z * 2 + y
+
+    def piece(g, cc, zz, yy):
+        if g == "a":
+            return r.wa.at[rows_of(64 * (cc * 8 + zz * 2 + yy), 64, 64), :]
+        if g == "f":
+            return r.wf.at[rows_of(64 * (cc * 8 + zz * 2 + yy), 64, 64), pl.ds(0, FH)]
+        if g == "s":
+            return r.wf.at[rows_of(64 * (cc * 8 + zz * 2 + yy), 64, 64), pl.ds(FH, FH)]
+        if g == "o":
+            return r.wo.at[rows_of(64 * (zz * 2 + yy), 64, 64), lanes_of(512 * cc, 512)]
+        return r.wd.at[rows_of(176 * (zz * 2 + yy), 176, 16), lanes_of(512 * cc, 512)]
+
+    def col_shard(g, who):
+        row = rows_of(64 * p + 32 * who, 32, 32)
+        if g == "a":
+            return r.wa.at[row, :]
+        return r.wf.at[row, pl.ds(0 if g == "f" else FH, FH)]
+
+    def start_cols(g):
+        gi = GROUPS.index(g)
+        if g == "a":
+            parts = [(w, HALF, HALF * j) for j, w in enumerate((r.wq, r.wk, r.wv, r.wg))]
+            full = r.wa
+        else:
+            parts = [(r.w1, FH, 0)] if g == "f" else [(r.w2, FH, FH)]
+            full = r.wf
+        row = rows_of(64 * p + 32 * x, 32, 32)
+        for w, width, at in parts:
+            local(w.at[:, lanes_of(width * x, width)], full.at[row, pl.ds(at, width)], r.s_wl.at[gi])
+            send(
+                w.at[:, lanes_of(width * (1 - x), width)], full.at[row, pl.ds(at, width)],
+                r.s_xs.at[gi, 0], r.s_xr.at[gi], xn, later=False,
+            )
+
+    def start_rows(g):
+        gi = GROUPS.index(g)
+        w = r.wo_in if g == "o" else r.wd_in
+
+        def place(h):
+            if g == "o":
+                return r.wo.at[rows_of(64 * m + 32 * x, 32, 32), lanes_of(512 * h, 512)]
+            return r.wds.at[x]
+
+        @pl.when(x == c)
+        def _():
+            local(w.at[:, lanes_of(512 * c, 512)], place(c), r.s_xr.at[gi])
+
+        @pl.when(x != c)
+        def _():
+            send(w.at[:, lanes_of(512 * c, 512)], place(c), r.s_xs.at[gi, 0], r.s_xr.at[gi], xn, later=False)
+
+        send(
+            w.at[:, lanes_of(512 * (1 - c), 512)], place(1 - c), r.s_xs.at[gi, 1], r.s_xr.at[gi], dev(1 - c, z, y, c),
+            later=False,
+        )
+
+    def piece_ready(g):
+        gi = GROUPS.index(g)
+        if g in ("a", "f", "s"):
+            own = col_shard(g, x)
+            pltpu.make_async_copy(own, own, r.s_wl.at[gi]).wait()
+            arrived(col_shard(g, 1 - x), r.s_xr.at[gi])
+        elif g == "o":
+            arrived(piece("o", c, z, y), r.s_xr.at[gi])
+        else:
+            arrived(r.wds, r.s_xr.at[gi])
+            both = jnp.concatenate([r.wds[0].astype(F32), r.wds[1].astype(F32)], axis=0)
+            r.wd[rows_of(176 * m, 176, 16), lanes_of(512 * c, 512)] = both.astype(BF16)
+
+    def spread_own(g):
+        gi = GROUPS.index(g)
+        piece_ready(g)
+        own = piece(g, c, z, y)
+        for k in (1, 3, 2):
+            send(own, own, r.s_zs.at[gi, k - 1], r.s_zr.at[gi, 3 - k], zp[k])
+        send(own, own, r.s_ys.at[gi, 0], r.s_yr.at[gi, 0], yn)
+        send(own, own, r.s_cs.at[gi, 0, 0], r.s_cr.at[gi, 0, 0], sib)
+
+    def spread_z(g):
+        gi = GROUPS.index(g)
+        for k in (1, 3, 2):
+            got = piece(g, c, zk[k], y)
+            arrived(got, r.s_zr.at[gi, k - 1])
+            send(got, got, r.s_ys.at[gi, k], r.s_yr.at[gi, k], yn)
+            send(got, got, r.s_cs.at[gi, k, 0], r.s_cr.at[gi, k, 0], sib)
+
+    def spread_y(g):
+        gi = GROUPS.index(g)
+        for k in (0, 1, 3, 2):
+            got = piece(g, c, zk[k], 1 - y)
+            arrived(got, r.s_yr.at[gi, k])
+            send(got, got, r.s_cs.at[gi, k, 1], r.s_cr.at[gi, k, 1], sib)
+
+    def whole(g):
+        gi = GROUPS.index(g)
+        for k in range(4):
+            for j in range(2):
+                arrived(piece(g, 1 - c, zk[k], y if j == 0 else 1 - y), r.s_cr.at[gi, k, j])
+
+    def swap(i, src, dst):
+        send(src, dst, r.s_es.at[i], r.s_er.at[i], xn)
+
+    def swapped(i, dst):
+        arrived(dst, r.s_er.at[i])
+
+    def sum_small(which, first):
+        base = 4 * which
+        r.gs[base] = first
+
+        def exchange(step, to, slot):
+            send(r.gs.at[base + step], r.gr.at[6 * which + slot], r.s_gs.at[which, slot], r.s_gr.at[which, slot], to)
+
+        def got(slot):
+            ref = r.gr.at[6 * which + slot]
+            arrived(ref, r.s_gr.at[which, slot])
+            return ref[...]
+
+        exchange(0, xn, 0)
+        total = first + got(0)
+        r.gs[base + 1] = total
+        exchange(1, yn, 1)
+        total = total + got(1)
+        r.gs[base + 2] = total
+        exchange(2, sib, 2)
+        total = total + got(2)
+        r.gs[base + 3] = total
+        for k in (1, 2, 3):
+            send(r.gs.at[base + 3], r.gr.at[6 * which + 2 + 4 - k], r.s_gs.at[which, 2 + k], r.s_gr.at[which, 6 - k], zp[k])
+        for k in (1, 2, 3):
+            total = total + got(2 + k)
+        return total
+
+    loads = [local(r.tokens, r.tok.at[pl.ds(0, OWN)], r.s_loc.at[0]), local(r.cot_in, r.cot.at[pl.ds(0, OWN)], r.s_loc.at[1])]
+    gain_load = local(r.gains, r.gr.at[12], r.s_loc.at[2])
+    start_cols("a")
+    swap(0, r.tokens, r.tok.at[pl.ds(OWN, OWN)])
+    start_rows("o")
+    start_cols("f")
+    start_cols("s")
+    start_rows("d")
+    swap(1, r.cot_in, r.cot.at[pl.ds(OWN, OWN)])
+
+    spread_own("a")
+    spread_own("o")
+    gain_load.wait()
+    gains = sum_small(0, r.gr[12])
+    r.gr[12] = gains
+    loads[0].wait()
+
+    def norm_rows(start):
+        rows = pl.ds(start, 64)
+        v = r.tok[rows, :].astype(F32)
+        scale = lax.rsqrt(jnp.mean(v * v, axis=-1, keepdims=True) + EPS)
+        r.nrm[rows, :] = (v * scale * r.gr[12, 0:1, :]).astype(BF16)
+
+    row_loop(OWN, 64, norm_rows)
+    swapped(0, r.tok.at[pl.ds(OWN, OWN)])
+    row_loop(OWN, 64, lambda s: norm_rows(s + OWN))
+    spread_z("a")
+    spread_own("f")
+    spread_y("a")
+    spread_z("o")
+    whole("a")
+
+    def proj(at, width):
+        r.qkv[:, pl.ds(at, width)] = dot(r.nrm[...], r.wa[:, pl.ds(at, width)]).astype(BF16)
+
+    def proj_gate(at, width):
+        r.gp[:, pl.ds(at, width)] = dot(r.nrm[...], r.wa[:, pl.ds(3 * HALF + at, width)])
+
+    tile_loop(3 * HALF, 256, proj)
+    tile_loop(HALF, 256, proj_gate)
+    spread_z("f")
+    spread_own("s")
+    spread_y("o")
+
+    lane = lax.broadcasted_iota(jnp.int32, (64, 128), 1)
+    row = lax.broadcasted_iota(jnp.int32, (64, 128), 0)
+    left = lane < 64
+    causal = (lane % 64) <= row
+
+    def pair(v):
+        zero = jnp.zeros_like(v)
+        return jnp.concatenate([jnp.where(left, v, zero), jnp.where(left, zero, v)], axis=0)
+
+    def half_sum(v):
+        zero = jnp.zeros_like(v)
+        a = jnp.sum(jnp.where(left, v, zero), axis=-1, keepdims=True)
+        b = jnp.sum(jnp.where(left, zero, v), axis=-1, keepdims=True)
+        return jnp.where(left, a, b)
+
+    def half_max(v):
+        low = jnp.full_like(v, -3e38)
+        a = jnp.max(jnp.where(left, v, low), axis=-1, keepdims=True)
+        b = jnp.max(jnp.where(left, low, v), axis=-1, keepdims=True)
+        return jnp.where(left, a, b)
+
+    def attend(start):
+        rows = pl.ds(start, 64)
+        for h in range(4):
+            cols = pl.ds(128 * h, 128)
+            q = r.qkv[rows, cols]
+            k = r.qkv[rows, pl.ds(HALF + 128 * h, 128)]
+            v = r.qkv[rows, pl.ds(2 * HALF + 128 * h, 128)]
+            s = jnp.where(causal, dot_t(q, pair(k)) * HDIM ** (-0.5), -1e30)
+            e = jnp.exp(s - half_max(s))
+            prob = e / half_sum(e)
+            r.prob[rows, cols] = prob
+            att = dot(prob.astype(BF16), pair(v))
+            r.att[rows, cols] = att
+            g = r.gp[rows, cols]
+            r.mix[rows, cols] = (att * (g * jax.nn.sigmoid(g))).astype(BF16)
+
+    row_loop(ROWS, 64, attend)
+    whole("o")
+
+    def split_store(acc, e, at, width):
+        r.po[:, pl.ds(at, width)] = acc[:OWN]
+        r.es[e, :, pl.ds(at, width)] = acc[OWN:].astype(BF16)
+
+    tile_loop(D, 256, lambda at, w: split_store(dot(r.mix[...], r.wo[:, pl.ds(at, w)]), 0, at, w))
+    swap(2, r.es.at[0], r.er.at[0])
+    spread_z("s")
+    spread_own("d")
+    spread_y("f")
+    swapped(2, r.er.at[0])
+
+    def resid_rows(start):
+        rows = pl.ds(start, 64)
+        v = r.tok[rows, :].astype(F32) + r.po[rows, :] + r.er[0, rows, :].astype(F32)
+        r.res[rows, :] = v
+        scale = lax.rsqrt(jnp.mean(v * v, axis=-1, keepdims=True) + EPS)
+        r.nt[rows, :] = (v * scale * r.gr[12, 1:2, :]).astype(BF16)
+
+    row_loop(OWN, 64, resid_rows)
+    swap(3, r.nt.at[pl.ds(0, OWN)], r.nt.at[pl.ds(OWN, OWN)])
+    spread_y("s")
+    spread_z("d")
+    whole("f")
+    whole("s")
+    swapped(3, r.nt.at[pl.ds(OWN, OWN)])
+
+    def hidden(at, width):
+        a = dot(r.nt[...], r.wf[:, pl.ds(at, width)]).astype(BF16)
+        b = dot(r.nt[...], r.wf[:, pl.ds(FH + at, width)]).astype(BF16)
+        r.fs[:, pl.ds(at, width)] = a
+        r.fs[:, pl.ds(FH + at, width)] = b
+        r.pr[:, pl.ds(at, width)] = (a.astype(F32) * b.astype(F32)).astype(BF16)
+
+    tile_loop(FH, 256, hidden)
+    loads[1].wait()
+    swapped(1, r.cot.at[pl.ds(OWN, OWN)])
+
+    def chunk_dot(i, cc):
+        kind, at, cols = CHUNKS[i]
+        if kind == "d":
+            out = t_dot(r.pr[...], r.cot[:, lanes_of(512 * cc + at, cols)])
+        elif kind == "f":
+            out = t_dot(r.nt[:, lanes_of(512 * cc, 512)], r.fs[:, pl.ds(at, cols)])
+        elif kind == "o":
+            out = t_dot(r.mix[...], r.bg[:, lanes_of(512 * cc, cols)])
+        else:
+            out = t_dot(r.nrm[:, lanes_of(512 * cc, 512)], r.g4[:, pl.ds(at, cols)])
+        return out.reshape(4, 2, piece_rows(kind), cols)
+
+    buf = lambda name, i: getattr(r, f"{name}{i}")
+    chunk_sends = {}
+
+    def give(i):
+        kind, _, cols = CHUNKS[i]
+        if i >= 4 and i - 2 in chunk_sends:
+            chunk_sends.pop(i - 2).wait_send()
+        stage = r.sbd.at[i % 2] if kind == "d" else r.sbf.at[i % 2, :, :, :, pl.ds(0, cols)]
+        stage[...] = chunk_dot(i, 1 - c).astype(BF16)
+        chunk_sends[i] = send(stage, buf("rb", i), r.r_cs.at[i], r.r_cr.at[i], sib, later=False)
+
+    def take(i):
+        arrived(buf("rb", i), r.r_cr.at[i])
+        own = buf("ow", i)
+        own[...] = (chunk_dot(i, c) + buf("rb", i)[...].astype(F32)).astype(BF16)
+        send(own.at[:, 1 - y], buf("yr", i), r.r_ys.at[i], r.r_yr.at[i], yn)
+
+    def take_y(i):
+        arrived(buf("yr", i), r.r_yr.at[i])
+        own, part = buf("ow", i), buf("yr", i)
+        for k in (1, 3, 2, 0):
+            slot = own.at[zk[k], y]
+            slot[...] = (slot[...].astype(F32) + part[zk[k]].astype(F32)).astype(BF16)
+            if k:
+                send(slot, buf("zr", i).at[3 - k], r.r_zs.at[i, k - 1], r.r_zr.at[i, 3 - k], zp[k])
+
+    finals = []
+
+    def take_z(i):
+        kind, at, cols = CHUNKS[i]
+        own, part, fin = buf("ow", i), buf("zr", i), buf("fin", i)
+        total = own[z, y].astype(F32)
+        for k in range(3):
+            arrived(part.at[k], r.r_zr.at[i, k])
+            total = total + part[k].astype(F32)
+        fin[...] = total
+        if kind in ("f", "a"):
+            if kind == "f":
+                out, place = (r.g1, FH * x + at) if at < FH else (r.g2, FH * x + at - FH)
+            else:
+                out, place = (r.gq, r.gk, r.gv, r.gg)[at // 512], HALF * x
+            dst = out.at[:, lanes_of(place, cols)]
+            finals.append(local(fin.at[rows_of(32 * x, 32, 32)], dst, r.r_fs.at[i, 0]))
+            send(fin.at[rows_of(32 * (1 - x), 32, 32)], dst, r.r_fs.at[i, 1], r.r_fr.at[i, 0], xn)
+            return
+        out = r.gd if kind == "d" else r.go
+        n = 88 if kind == "d" else 32
+        dst = out.at[:, lanes_of(512 * c + at, cols)]
+        for xx in range(2):
+            src = fin.at[pl.ds(n * xx, n)]
+            itself = jnp.logical_and(x == c, x == xx)
+
+            @pl.when(itself)
+            def _():
+                local(src, dst, r.r_fr.at[i, c])
+
+            @pl.when(jnp.logical_not(itself))
+            def _():
+                send(src, dst, r.r_fs.at[i, xx], r.r_fr.at[i, c], dev(x, z, y, xx), later=False)
+
+    def finish(i):
+        kind, at, cols = CHUNKS[i]
+        if kind in ("f", "a"):
+            if kind == "f":
+                out, place = (r.g1, FH * (1 - x) + at) if at < FH else (r.g2, FH * (1 - x) + at - FH)
+            else:
+                out, place = (r.gq, r.gk, r.gv, r.gg)[at // 512], HALF * (1 - x)
+            arrived(out.at[:, lanes_of(place, cols)], r.r_fr.at[i, 0])
+            return
+        out = r.gd if kind == "d" else r.go
+        n = 88 if kind == "d" else 32
+        for cc in range(2):
+            arrived(out.at[:, pl.ds(512 * cc + at, cols)], r.r_fr.at[i, cc])
+        for xx in range(2):
+            itself = jnp.logical_and(x == c, x == xx)
+
+            @pl.when(jnp.logical_not(itself))
+            def _():
+                src = buf("fin", i).at[pl.ds(n * xx, n)]
+                remote(src, src, r.r_fs.at[i, xx], r.r_fs.at[i, xx], xn).wait_send()
+
+    give(0)
+    spread_y("d")
+    give(1)
+    take(0)
+    whole("d")
+
+    def hidden_grad(at, width):
+        pg = dot_t(r.cot[...], r.wd[pl.ds(at, width), :]).astype(BF16).astype(F32)
+        a = r.fs[:, pl.ds(at, width)].astype(F32)
+        b = r.fs[:, pl.ds(FH + at, width)].astype(F32)
+        r.fs[:, pl.ds(at, width)] = (pg * b).astype(BF16)
+        r.fs[:, pl.ds(FH + at, width)] = (pg * a).astype(BF16)
+
+    tile_loop(FH, 256, hidden_grad)
+    tile_loop(D, 256, lambda at, w: split_store(dot_t(r.fs[...], r.wf[pl.ds(at, w), :]), 1, at, w))
+    swap(4, r.es.at[1], r.er.at[1])
+    take(1)
+    give(2)
+    take_y(0)
+    give(3)
+    take(2)
+    swapped(4, r.er.at[1])
+    r.gacc[...] = jnp.zeros((2, 8, D), F32)
+
+    def resid_grad_rows(start):
+        rows = pl.ds(start, 64)
+        ng = r.po[rows, :] + r.er[1, rows, :].astype(F32)
+        v = r.res[rows, :]
+        scale = lax.rsqrt(jnp.mean(v * v, axis=-1, keepdims=True) + EPS)
+        n = ng * r.gr[12, 1:2, :]
+        grad = r.cot[rows, :].astype(F32) + scale * n - v * (scale * scale * scale * jnp.mean(n * v, axis=-1, keepdims=True))
+        r.rg[rows, :] = grad
+        r.bg[rows, :] = grad.astype(BF16)
+        r.gacc[1] += jnp.sum((ng * v * scale).reshape(8, 8, D), axis=0)
+
+    row_loop(OWN, 64, resid_grad_rows)
+    swap(5, r.bg.at[pl.ds(0, OWN)], r.bg.at[pl.ds(OWN, OWN)])
+    tile_loop(D, 256, lambda at, w: split_store(dot(r.pr[...], r.wd[:, pl.ds(at, w)]), 3, at, w))
+    swap(6, r.es.at[3], r.er.at[3])
+    take_y(1)
+    give(4)
+    take(3)
+    take_z(0)
+    swapped(5, r.bg.at[pl.ds(OWN, OWN)])
+
+    def mixed_grad(at, width):
+        cols = pl.ds(at, width)
+        mg = dot_t(r.bg[...], r.wo[pl.ds(at, width), :]).astype(BF16).astype(F32)
+        g = r.gp[:, cols]
+        s = jax.nn.sigmoid(g)
+        r.dout[:, cols] = (mg * (g * s)).astype(BF16)
+        r.g4[:, pl.ds(3 * HALF + at, width)] = (mg * r.att[:, cols] * (s * (1.0 + g * (1.0 - s)))).astype(BF16)
+
+    tile_loop(HALF, 256, mixed_grad)
+
+    def attend_grad(start):
+        rows = pl.ds(start, 64)
+        for h in range(4):
+            cols = pl.ds(128 * h, 128)
+            q = r.qkv[rows, cols]
+            k = r.qkv[rows, pl.ds(HALF + 128 * h, 128)]
+            v = r.qkv[rows, pl.ds(2 * HALF + 128 * h, 128)]
+            do = r.dout[rows, cols]
+            prob = r.prob[rows, cols]
+            vg = t_dot(prob.astype(BF16), do)
+            r.g4[rows, pl.ds(2 * HALF + 128 * h, 128)] = jnp.where(left, vg[:64], vg[64:]).astype(BF16)
+            pg = dot_t(do, pair(v))
+            sg = (prob * (pg - half_sum(prob * pg))).astype(BF16)
+            r.g4[rows, cols] = (dot(sg, pair(k)) * HDIM ** (-0.5)).astype(BF16)
+            kg = t_dot(sg, q)
+            r.g4[rows, pl.ds(HALF + 128 * h, 128)] = (jnp.where(left, kg[:64], kg[64:]) * HDIM ** (-0.5)).astype(BF16)
+
+    row_loop(ROWS, 64, attend_grad)
+    swapped(6, r.er.at[3])
+
+    def block_out_rows(start):
+        rows = pl.ds(start, 64)
+        r.bo[rows, :] = (r.res[rows, :] + r.po[rows, :] + r.er[3, rows, :].astype(F32)).astype(BF16)
+
+    row_loop(OWN, 64, block_out_rows)
+    outs = [local(r.bo, r.block_out, r.s_out.at[0])]
+    tile_loop(D, 256, lambda at, w: split_store(dot_t(r.g4[...], r.wa[pl.ds(at, w), :]), 2, at, w))
+    swap(7, r.es.at[2], r.er.at[2])
+    take_y(2)
+    give(5)
+    take(4)
+    take_z(1)
+    swapped(7, r.er.at[2])
+
+    def tokens_grad_rows(start):
+        rows = pl.ds(start, 64)
+        ng = r.po[rows, :] + r.er[2, rows, :].astype(F32)
+        v = r.tok[rows, :].astype(F32)
+        scale = lax.rsqrt(jnp.mean(v * v, axis=-1, keepdims=True) + EPS)
+        n = ng * r.gr[12, 0:1, :]
+        r.rg[rows, :] = r.rg[rows, :] + scale * n - v * (scale * scale * scale * jnp.mean(n * v, axis=-1, keepdims=True))
+        r.gacc[0] += jnp.sum((ng * v * scale).reshape(8, 8, D), axis=0)
+
+    row_loop(OWN, 64, tokens_grad_rows)
+    outs.append(local(r.rg, r.tokens_grad, r.s_out.at[1]))
+    take_y(3)
+    give(6)
+    take(5)
+    for i in range(7, NCH + 4):
+        if i < NCH:
+            give(i)
+        if i - 1 < NCH:
+            take(i - 1)
+        if 0 <= i - 3 < NCH:
+            take_y(i - 3)
+        if 0 <= i - 5 < NCH:
+            take_z(i - 5)
+        if i == NCH:
+            which = lax.broadcasted_iota(jnp.int32, (8, D), 0)
+            a = jnp.sum(r.gacc[0], axis=0, keepdims=True)
+            b = jnp.sum(r.gacc[1], axis=0, keepdims=True)
+            zero = jnp.zeros((8, D), F32)
+            total = sum_small(1, jnp.where(which == 0, a, zero) + jnp.where(which == 1, b, zero))
+            r.gacc[0] = total
+            outs.append(local(r.gacc.at[0], r.gain_grads, r.s_out.at[2]))
+    take_z(NCH - 1)
+    for i in range(NCH):
+        finish(i)
+    for copy in list(chunk_sends.values()) + sends:
+        copy.wait_send()
+    for copy in finals + outs:
+        copy.wait()
+    for g in ("a", "f", "s"):
+        gi = GROUPS.index(g)
+        own = col_shard(g, x)
+        remote(own, own, r.s_xs.at[gi, 0], r.s_xs.at[gi, 0], xn).wait_send()
+    for g in ("o", "d"):
+        gi = GROUPS.index(g)
+        block = r.wo.at[pl.ds(0, 32), pl.ds(0, 512)] if g == "o" else r.wds.at[0]
+
+        @pl.when(x != c)
+        def _():
+            remote(block, block, r.s_xs.at[gi, 0], r.s_xs.at[gi, 0], xn).wait_send()
+
+        remote(block, block, r.s_xs.at[gi, 1], r.s_xs.at[gi, 1], xn).wait_send()
+
+
+def fused_layer(
+    tokens, attn_gain, w_query, w_key, w_value, w_gate, w_output, ffn_gain, w_first, w_second, w_down, cotangent
+):
+    me = lax.axis_index("dp") * 16 + lax.axis_index("fsdp")
+    lane = lax.broadcasted_iota(jnp.int32, (8, D), 1)
+    row = lax.broadcasted_iota(jnp.int32, (8, D), 0)
+    mine = lane // 32 == me
+    spread = lambda gain: jnp.tile(gain.astype(F32), 32)[None, :]
+    gains = jnp.where(mine & (row == 0), spread(attn_gain), 0.0) + jnp.where(mine & (row == 1), spread(ffn_gain), 0.0)
+    items = scratch_list()
+    names = IN_NAMES + OUT_NAMES + tuple(name for name, _ in items)
+    shape = jax.ShapeDtypeStruct
+    outs = pl.pallas_call(
+        functools.partial(layer_kernel, names),
+        out_shape=[
+            shape((OWN, D), BF16), shape((OWN, D), F32), shape((8, D), F32),
+            shape((32, D), F32), shape((32, D), F32), shape((32, D), F32), shape((32, D), F32), shape((32, D), F32),
+            shape((32, FF), F32), shape((32, FF), F32), shape((88, D), F32),
+        ],
+        in_specs=[pl.BlockSpec(memory_space=pl.ANY)] * len(IN_NAMES),
+        out_specs=[pl.BlockSpec(memory_space=pl.ANY)] * len(OUT_NAMES),
+        scratch_shapes=[spec for _, spec in items],
+        compiler_params=pltpu.CompilerParams(collective_id=0, has_side_effects=True, vmem_limit_bytes=66 * 2**20 - 2**21),
+        name="layer",
+    )(tokens, gains, w_query, w_key, w_value, w_gate, w_output, w_first, w_second, w_down, cotangent)
+    block_out, tokens_grad, gain_grads, gq, gk, gv, gg, go, g1, g2, gd = outs
+    own = lax.dynamic_slice(gain_grads, (0, me * 32), (8, 32))
+    return block_out, tokens_grad, own[0], gq, gk, gv, gg, go, own[1], g1, g2, gd
 
 
 def rms_scale(values, gain):
@@ -254,8 +919,9 @@
 
 
 def solution(mesh):
+    fits = dict(mesh.shape) == {"dp": 2, "fsdp": 16}
     return jax.shard_map(
-        on_device,
+        fused_layer if fits else on_device,
         mesh=mesh,
         in_specs=(
             P(("dp", "fsdp"), None),

time: 2040 us -> 266 us (0.13)
  waiting for transfers between devices: 1710 us -> 0 us
  Pallas kernels: 0 us -> 251 us
  local copies, waits for them, and re-layouts: 115 us -> 12.8 us
  matrix products: 98.8 us -> 0 us
  blocking collectives: 83 us -> 0 us
    reduce_scatter x8 -> x0, waiting for transfers between devices: 1300 us -> none  [the longest x1 251 us: on_device(): lax.psum_scatter(flatten_rows(first_w_grad), ('dp', 'fsdp'), scatter_dime...]
    all_gather x8 -> x0, waiting for transfers between devices: 407 us -> none  [the longest x1 65.3 us: on_device(): lax.all_gather(w_second, ('dp', 'fsdp'), axis=0, tiled=True)]
    pallas_call x0 -> x1, Pallas kernels: none -> 251 us  [fused_layer(): pl.pallas_call(functools.partial(layer_kernel, names), out_shape=[shape((...]
    dot_general x30 -> x0, matrix products: 98.8 us -> none  [the longest x8 34.6 us: contract_rows(): lax.dot_general(left, right, (((0,), (0,)), ((), ())), preferred_element_...]
    reshape x24 -> x0, local copies, waits for them, and re-layouts: 90.2 us -> none  [the longest x8 63.1 us: flatten_rows(): return matrix.reshape(-1, 128)]
    unnamed x2 -> x0, blocking collectives: 83 us -> none
  transfers between devices with their start and end apart: 16 -> 0, of which waited for: 15 -> 0; matrix products, arithmetic and copies ran while one was open for 9% -> 0% of each run, Pallas kernels for 0% -> 0%
where the time goes in v2:
time: 266 us; the launch traced here: 265 us
  Pallas kernels  251 us (94%)
  local copies, waits for them, and re-layouts  12.8 us (5%)
    pallas_call x1, Pallas kernels, fused_layer(): pl.pallas_call(functools.partial(layer_kernel, names), out_shape=[shape((...  251 us
    unnamed x32, local copies, waits for them, and re-layouts  11.3 us

profile of v2, /device:TPU:0, one launch (start us, length us, event | category | flops | bytes accessed | tf_op | source)
XLA Modules:
  0.0 265.2 jit_solution(9944984396131376677)
XLA Ops:
  0.7 0.6 copy-done.9
  1.4 0.1 broadcast_in_dim.22
  1.4 0.6 copy-done.10
  2.0 0.1 broadcast_in_dim.25
  2.1 0.7 select_add_fusion.refs_1_
  2.8 251.0 %layer.1 = (bf16[256,1024]{1,0:T(8,128)(2,1)}, f32[256,1024]{1,0:T(8,128)}, f32[8,1024]{1,0:T(8,128)}, f32[32,1024]{1,0:T(8,128)}, f32[32,1024]{1,0:T(8,128)}, /...) custom-call(bf16[256,1024]{1,0:T(8,128)(2,1)} %refs_0_.1, ...), custom_call_target="tpu_custom_call" | custom-call | tf_op jit(solution)/shard_map/layer/pallas_call | solution.py:663
  253.8 0.8 constant_dynamic-slice_fusion
  254.6 0.5 slice_bitcast_fusion
  255.2 1.9 copy.34
  257.0 1.0 copy.35
  258.0 0.1 copy-done.8
  258.1 0.7 copy.36
  258.7 0.3 copy-done.7
  259.0 0.7 copy.37
  259.7 0.3 copy-done.6
  260.0 0.7 copy.38
  260.6 0.7 copy.39
  261.3 0.3 copy-done.4
  261.6 0.7 copy.40
  262.2 0.7 copy.41
  263.0 0.4 copy-done.2
  263.4 0.7 copy.42
  264.1 0.4 copy-done.1
  264.5 0.7 copy.43
  (19 shorter events, 0.1 us)
Async XLA Ops:
  0.7 0.7 copy-start.9
  1.3 0.7 copy-start.10
  253.8 3.2 %copy-start = (f32[256,1024]{1,0:T(8,128)S(1)}, f32[256,1024]{1,0:T(8,128)}, u32[]{:S(2)}) copy-start(f32[256,1024]{1,0:T(8,128)} %get-tuple-element.53) | copy-start | bytes 3145732
  257.0 1.0 copy-start.8
  258.1 1.0 copy-start.7
  259.0 1.0 copy-start.6
  259.0 1.6 copy-start.5
  260.0 2.3 copy-start.3
  260.6 1.0 copy-start.4
  262.2 1.1 copy-start.2
  263.3 1.1 copy-start.1

commit v3 on v2

--- a/solution.py
+++ b/solution.py
@@ -28,10 +28,13 @@
     ("d", 0, 256), ("d", 256, 256),
     ("f", 0, 768), ("f", 768, 640), ("f", 1408, 768), ("f", 2176, 640),
     ("o", 0, 512),
-    ("a", 0, 512), ("a", 512, 512), ("a", 1024, 512), ("a", 1536, 512),
+    ("a", 1536, 512), ("a", 1024, 512), ("a", 512, 512), ("a", 0, 512),
 )
 NCH = len(CHUNKS)
-GROUPS = ("a", "o", "f", "s", "d")
+Z_FIRST = tuple(i in (1, 7,) for i in range(NCH))
+Y_FIRST = ("d",)
+GROUPS = ("a", "b", "o", "f", "s", "d")
+GA, GB, GO, GF, GS, GD = GROUPS
 
 
 def piece_rows(kind):
@@ -41,7 +44,7 @@
 def scratch_list():
     vm, dma = pltpu.VMEM, pltpu.SemaphoreType.DMA
     items = [
-        ("wa", vm((D, 4 * HALF), BF16)), ("wf", vm((D, 2 * FH), BF16)),
+        ("wa", vm((D, 4 * HALF + 128), BF16)), ("wf", vm((D, 2 * FH), BF16)),
         ("wo", vm((HALF, D), BF16)), ("wd", vm((FH, D), BF16)), ("wds", vm((2, 88, 512), BF16)),
         ("tok", vm((ROWS, D), BF16)), ("cot", vm((ROWS, D), BF16)), ("nrm", vm((ROWS, D), BF16)),
         ("qkv", vm((ROWS, 3 * HALF), BF16)), ("gp", vm((ROWS, HALF), F32)), ("att", vm((ROWS, HALF), F32)),
@@ -49,26 +52,28 @@
         ("res", vm((OWN, D), F32)), ("nt", vm((ROWS, D), BF16)), ("fs", vm((ROWS, 2 * FH), BF16)),
         ("pr", vm((ROWS, FH), BF16)), ("g4", vm((ROWS, 4 * HALF), BF16)), ("bg", vm((ROWS, D), BF16)),
         ("rg", vm((OWN, D), F32)), ("po", vm((OWN, D), F32)), ("bo", vm((OWN, D), BF16)),
-        ("es", vm((4, OWN, D), BF16)), ("er", vm((4, OWN, D), BF16)),
-        ("gs", vm((8, 8, D), F32)), ("gr", vm((13, 8, D), F32)), ("gacc", vm((2, 8, D), F32)),
+        ("es", vm((3, OWN, D), BF16)), ("er", vm((3, OWN, D), BF16)),
+        ("gs", vm((4, 8, D), F32)), ("gr", vm((6, 8, D), F32)), ("gain", vm((8, D), F32)), ("gacc", vm((2, 8, D), F32)),
         ("sbd", vm((2, 4, 2, 176, 256), BF16)), ("sbf", vm((2, 4, 2, 64, 768), BF16)),
     ]
     for i, (kind, _, cols) in enumerate(CHUNKS):
         r = piece_rows(kind)
         items += [
             (f"rb{i}", vm((4, 2, r, cols), BF16)), (f"ow{i}", vm((4, 2, r, cols), BF16)),
-            (f"yr{i}", vm((4, r, cols), BF16)), (f"zr{i}", vm((3, r, cols), BF16)),
+            (f"yr{i}", vm((r, cols) if Z_FIRST[i] else (4, r, cols), BF16)),
+            (f"zr{i}", vm((3, 2, r, cols) if Z_FIRST[i] else (3, r, cols), BF16)),
+            (f"zx{i}", vm((2, r, cols) if Z_FIRST[i] else (r, cols), BF16)),
             (f"fin{i}", vm((r, cols), F32)),
         ]
     n = len(GROUPS)
     items += [
         ("s_loc", dma((4,))), ("s_wl", dma((n,))), ("s_xs", dma((n, 2))), ("s_xr", dma((n,))),
-        ("s_es", dma((8,))), ("s_er", dma((8,))),
-        ("s_zs", dma((n, 3))), ("s_zr", dma((n, 3))), ("s_ys", dma((n, 4))), ("s_yr", dma((n, 4))),
+        ("s_es", dma((16,))), ("s_er", dma((16,))),
+        ("s_zs", dma((n, 2, 5))), ("s_zr", dma((n, 2, 3))), ("s_ys", dma((n, 4))), ("s_yr", dma((n, 4))),
         ("s_cs", dma((n, 4, 2))), ("s_cr", dma((n, 4, 2))),
-        ("s_gs", dma((2, 6))), ("s_gr", dma((2, 6))),
+        ("s_gs", dma((6,))), ("s_gr", dma((6,))),
         ("r_cs", dma((NCH,))), ("r_cr", dma((NCH,))), ("r_ys", dma((NCH,))), ("r_yr", dma((NCH,))),
-        ("r_zs", dma((NCH, 3))), ("r_zr", dma((NCH, 3))), ("r_fs", dma((NCH, 2))), ("r_fr", dma((NCH, 2))),
+        ("r_zs", dma((NCH, 3))), ("r_zr", dma((NCH, 3))), ("r_zx", dma((NCH,))), ("r_zt", dma((NCH,))), ("r_fs", dma((NCH, 2))), ("r_fr", dma((NCH, 2))),
         ("s_out", dma((4,))),
     ]
     return items
@@ -135,7 +140,8 @@
         pl.semaphore_signal(barrier, inc=1, device_id=peer, device_id_type=MESH)
     pl.semaphore_wait(barrier, 7)
 
-    sends = []
+    sends, guarded = [], []
+    inner = jnp.logical_and(z != 0, z != 3)
 
     def remote(src, dst, ss, rs, to):
         return pltpu.make_async_remote_copy(
@@ -149,6 +155,11 @@
             sends.append(copy)
         return copy
 
+    def send_if(pred, src, dst, ss, rs, to):
+        copy = remote(src, dst, ss, rs, to)
+        pl.when(pred)(copy.start)
+        guarded.append((pred, copy))
+
     def arrived(ref, sem):
         remote(ref, ref, sem, sem, xn).wait_recv()
 
@@ -162,8 +173,9 @@
     m = z * 2 + y
 
     def piece(g, cc, zz, yy):
-        if g == "a":
-            return r.wa.at[rows_of(64 * (cc * 8 + zz * 2 + yy), 64, 64), :]
+        if g in "ab":
+            cols = pl.ds(0, 1024) if g == "a" else pl.ds(1024, 1024 + 128)
+            return r.wa.at[rows_of(64 * (cc * 8 + zz * 2 + yy), 64, 64), cols]
         if g == "f":
             return r.wf.at[rows_of(64 * (cc * 8 + zz * 2 + yy), 64, 64), pl.ds(0, FH)]
         if g == "s":
@@ -174,19 +186,23 @@
 
     def col_shard(g, who):
         row = rows_of(64 * p + 32 * who, 32, 32)
-        if g == "a":
-            return r.wa.at[row, :]
+        if g in "ab":
+            return r.wa.at[row, pl.ds(0, 1024) if g == "a" else pl.ds(1024, 1024 + 128)]
         return r.wf.at[row, pl.ds(0 if g == "f" else FH, FH)]
 
     def start_cols(g):
         gi = GROUPS.index(g)
-        if g == "a":
-            parts = [(w, HALF, HALF * j) for j, w in enumerate((r.wq, r.wk, r.wv, r.wg))]
+        if g in "ab":
+            first = 0 if g == "a" else 2
+            parts = [(w, HALF, HALF * j) for j, w in enumerate((r.wq, r.wk, r.wv, r.wg))][first : first + 2]
             full = r.wa
         else:
             parts = [(r.w1, FH, 0)] if g == "f" else [(r.w2, FH, FH)]
             full = r.wf
         row = rows_of(64 * p + 32 * x, 32, 32)
+        if g == "b":
+            local(r.gains, full.at[row, pl.ds(4 * HALF, 128)], r.s_wl.at[gi])
+            send(r.gains, full.at[row, pl.ds(4 * HALF, 128)], r.s_xs.at[gi, 0], r.s_xr.at[gi], xn, later=False)
         for w, width, at in parts:
             local(w.at[:, lanes_of(width * x, width)], full.at[row, pl.ds(at, width)], r.s_wl.at[gi])
             send(
@@ -218,7 +234,7 @@
 
     def piece_ready(g):
         gi = GROUPS.index(g)
-        if g in ("a", "f", "s"):
+        if g in "abfs":
             own = col_shard(g, x)
             pltpu.make_async_copy(own, own, r.s_wl.at[gi]).wait()
             arrived(col_shard(g, 1 - x), r.s_xr.at[gi])
@@ -229,112 +245,119 @@
             both = jnp.concatenate([r.wds[0].astype(F32), r.wds[1].astype(F32)], axis=0)
             r.wd[rows_of(176 * m, 176, 16), lanes_of(512 * c, 512)] = both.astype(BF16)
 
-    def spread_own(g):
+    near = [
+        jnp.where(z < 2, 1, 3),
+        jnp.where(z == 1, 3, jnp.where(z == 2, 1, 2)),
+        jnp.where(z == 0, 3, jnp.where(z == 3, 1, 2)),
+    ]
+
+    def near_z(n):
+        return z if n == 0 else lax.rem(z + near[n - 1], 4)
+
+    def up_down(g, yy, j):
         gi = GROUPS.index(g)
+        own = piece(g, c, z, yy)
+        send_if(z < 3, own, own, r.s_zs.at[gi, j, 0], r.s_zr.at[gi, j, 2], zp[1])
+        send_if(z > 0, own, own, r.s_zs.at[gi, j, 1], r.s_zr.at[gi, j, 0], zp[3])
+
+    def across(g, n):
+        gi = GROUPS.index(g)
+        ref = piece(g, c, near_z(n), y)
+        send(ref, ref, r.s_ys.at[gi, n], r.s_yr.at[gi, n], yn)
+
+    def to_core(g, n, j):
+        gi = GROUPS.index(g)
+        ref = piece(g, c, near_z(n), y if j == 0 else 1 - y)
+        send(ref, ref, r.s_cs.at[gi, n, j], r.s_cr.at[gi, n, j], sib)
+
+    def own(g):
         piece_ready(g)
-        own = piece(g, c, z, y)
-        for k in (1, 3, 2):
-            send(own, own, r.s_zs.at[gi, k - 1], r.s_zr.at[gi, 3 - k], zp[k])
-        send(own, own, r.s_ys.at[gi, 0], r.s_yr.at[gi, 0], yn)
-        send(own, own, r.s_cs.at[gi, 0, 0], r.s_cr.at[gi, 0, 0], sib)
+        if g in Y_FIRST:
+            across(g, 0)
+            up_down(g, y, 0)
+        else:
+            up_down(g, y, 0)
+            across(g, 0)
+        to_core(g, 0, 0)
+
+    def got_z(g, n, j=0):
+        gi = GROUPS.index(g)
+        got = piece(g, c, near_z(n), y if j == 0 else 1 - y)
+        arrived(got, r.s_zr.at[gi, j, near[n - 1] - 1])
+        src = near_z(n)
+        to = jnp.where(src > z, z - 1, z + 1)
+        slot = lax.rem(src - to + 4, 4) - 1
+        send_if(inner, got, got, r.s_zs.at[gi, j, 1 + n], r.s_zr.at[gi, j, slot], dev(c, to, y, x))
+        if g not in Y_FIRST:
+            across(g, n)
+        to_core(g, n, j)
+
+    def got_y(g, n):
+        gi = GROUPS.index(g)
+        arrived(piece(g, c, near_z(n), 1 - y), r.s_yr.at[gi, n])
+        if g in Y_FIRST:
+            up_down(g, 1 - y, 1)
+        to_core(g, n, 1)
 
     def spread_z(g):
-        gi = GROUPS.index(g)
-        for k in (1, 3, 2):
-            got = piece(g, c, zk[k], y)
-            arrived(got, r.s_zr.at[gi, k - 1])
-            send(got, got, r.s_ys.at[gi, k], r.s_yr.at[gi, k], yn)
-            send(got, got, r.s_cs.at[gi, k, 0], r.s_cr.at[gi, k, 0], sib)
+        for j in range(2 if g in Y_FIRST else 1):
+            for n in (1, 2, 3):
+                got_z(g, n, j)
 
     def spread_y(g):
-        gi = GROUPS.index(g)
-        for k in (0, 1, 3, 2):
-            got = piece(g, c, zk[k], 1 - y)
-            arrived(got, r.s_yr.at[gi, k])
-            send(got, got, r.s_cs.at[gi, k, 1], r.s_cr.at[gi, k, 1], sib)
+        for n in range(1 if g in Y_FIRST else 4):
+            got_y(g, n)
 
     def whole(g):
         gi = GROUPS.index(g)
         for k in range(4):
             for j in range(2):
-                arrived(piece(g, 1 - c, zk[k], y if j == 0 else 1 - y), r.s_cr.at[gi, k, j])
+                arrived(piece(g, 1 - c, near_z(k), y if j == 0 else 1 - y), r.s_cr.at[gi, k, j])
+
+    swaps = {}
 
     def swap(i, src, dst):
-        send(src, dst, r.s_es.at[i], r.s_er.at[i], xn)
+        swaps[i] = send(src, dst, r.s_es.at[i], r.s_er.at[i], xn, later=False)
 
     def swapped(i, dst):
         arrived(dst, r.s_er.at[i])
 
-    def sum_small(which, first):
-        base = 4 * which
-        r.gs[base] = first
-
-        def exchange(step, to, slot):
-            send(r.gs.at[base + step], r.gr.at[6 * which + slot], r.s_gs.at[which, slot], r.s_gr.at[which, slot], to)
+    def grad_sum(n, value=None):
+        def out(slot, to):
+            send(r.gs.at[min(slot, 3)], r.gr.at[slot], r.s_gs.at[slot], r.s_gr.at[slot], to)
 
         def got(slot):
-            ref = r.gr.at[6 * which + slot]
-            arrived(ref, r.s_gr.at[which, slot])
-            return ref[...]
-
-        exchange(0, xn, 0)
-        total = first + got(0)
-        r.gs[base + 1] = total
-        exchange(1, yn, 1)
-        total = total + got(1)
-        r.gs[base + 2] = total
-        exchange(2, sib, 2)
-        total = total + got(2)
-        r.gs[base + 3] = total
-        for k in (1, 2, 3):
-            send(r.gs.at[base + 3], r.gr.at[6 * which + 2 + 4 - k], r.s_gs.at[which, 2 + k], r.s_gr.at[which, 6 - k], zp[k])
-        for k in (1, 2, 3):
-            total = total + got(2 + k)
-        return total
-
-    loads = [local(r.tokens, r.tok.at[pl.ds(0, OWN)], r.s_loc.at[0]), local(r.cot_in, r.cot.at[pl.ds(0, OWN)], r.s_loc.at[1])]
-    gain_load = local(r.gains, r.gr.at[12], r.s_loc.at[2])
-    start_cols("a")
-    swap(0, r.tokens, r.tok.at[pl.ds(OWN, OWN)])
-    start_rows("o")
-    start_cols("f")
-    start_cols("s")
-    start_rows("d")
-    swap(1, r.cot_in, r.cot.at[pl.ds(OWN, OWN)])
-
-    spread_own("a")
-    spread_own("o")
-    gain_load.wait()
-    gains = sum_small(0, r.gr[12])
-    r.gr[12] = gains
-    loads[0].wait()
-
-    def norm_rows(start):
+            arrived(r.gr.at[slot], r.s_gr.at[slot])
+            return r.gr[slot]
+
+        if n == 0:
+            r.gs[0] = value
+            out(0, xn)
+        elif n < 3:
+            r.gs[n] = r.gs[n - 1] + got(n - 1)
+            out(n, yn if n == 1 else sib)
+        elif n == 3:
+            r.gs[3] = r.gs[2] + got(2)
+            for k in (1, 2, 3):
+                send(r.gs.at[3], r.gr.at[6 - k], r.s_gs.at[2 + k], r.s_gr.at[6 - k], zp[k])
+        else:
+            return r.gs[3] + (got(3) + got(4) + got(5))
+
+    def norm_rows(start, at, out):
+        v = r.tok[pl.ds(start + at, 64), :].astype(F32)
+        scale = lax.rsqrt(jnp.mean(v * v, axis=-1, keepdims=True) + EPS)
+        out[pl.ds(start, 64), :] = v * scale
+
+    def gain_rows(start):
         rows = pl.ds(start, 64)
-        v = r.tok[rows, :].astype(F32)
-        scale = lax.rsqrt(jnp.mean(v * v, axis=-1, keepdims=True) + EPS)
-        r.nrm[rows, :] = (v * scale * r.gr[12, 0:1, :]).astype(BF16)
-
-    row_loop(OWN, 64, norm_rows)
-    swapped(0, r.tok.at[pl.ds(OWN, OWN)])
-    row_loop(OWN, 64, lambda s: norm_rows(s + OWN))
-    spread_z("a")
-    spread_own("f")
-    spread_y("a")
-    spread_z("o")
-    whole("a")
+        r.nrm[rows, :] = (r.po[rows, :] * r.gain[0:1, :]).astype(BF16)
+        r.nrm[pl.ds(start + OWN, 64), :] = (r.rg[rows, :] * r.gain[0:1, :]).astype(BF16)
 
     def proj(at, width):
         r.qkv[:, pl.ds(at, width)] = dot(r.nrm[...], r.wa[:, pl.ds(at, width)]).astype(BF16)
 
     def proj_gate(at, width):
         r.gp[:, pl.ds(at, width)] = dot(r.nrm[...], r.wa[:, pl.ds(3 * HALF + at, width)])
-
-    tile_loop(3 * HALF, 256, proj)
-    tile_loop(HALF, 256, proj_gate)
-    spread_z("f")
-    spread_own("s")
-    spread_y("o")
 
     lane = lax.broadcasted_iota(jnp.int32, (64, 128), 1)
     row = lax.broadcasted_iota(jnp.int32, (64, 128), 0)
@@ -373,34 +396,33 @@
             g = r.gp[rows, cols]
             r.mix[rows, cols] = (att * (g * jax.nn.sigmoid(g))).astype(BF16)
 
-    row_loop(ROWS, 64, attend)
-    whole("o")
-
-    def split_store(acc, e, at, width):
-        r.po[:, pl.ds(at, width)] = acc[:OWN]
-        r.es[e, :, pl.ds(at, width)] = acc[OWN:].astype(BF16)
-
-    tile_loop(D, 256, lambda at, w: split_store(dot(r.mix[...], r.wo[:, pl.ds(at, w)]), 0, at, w))
-    swap(2, r.es.at[0], r.er.at[0])
-    spread_z("s")
-    spread_own("d")
-    spread_y("f")
-    swapped(2, r.er.at[0])
+    def partial_rows(left, right, slot, start, count):
+        rows = pl.ds(start, count)
+
+        def tile(at, width):
+            acc = right(left[rows, :], at, width)
+            if start < OWN:
+                r.po[rows, pl.ds(at, width)] = acc
+            else:
+                r.es[slot, pl.ds(start - OWN, count), pl.ds(at, width)] = acc.astype(BF16)
+
+        tile_loop(D, 256, tile)
+
+    def out_product(v, at, width):
+        return dot(v, r.wo[:, pl.ds(at, width)])
+
+    def hidden_back(v, at, width):
+        return dot_t(v, r.wf[pl.ds(at, width), :])
+
+    def heads_back(v, at, width):
+        return dot_t(v, r.wa[pl.ds(at, width), pl.ds(0, 4 * HALF)])
 
     def resid_rows(start):
         rows = pl.ds(start, 64)
         v = r.tok[rows, :].astype(F32) + r.po[rows, :] + r.er[0, rows, :].astype(F32)
         r.res[rows, :] = v
         scale = lax.rsqrt(jnp.mean(v * v, axis=-1, keepdims=True) + EPS)
-        r.nt[rows, :] = (v * scale * r.gr[12, 1:2, :]).astype(BF16)
-
-    row_loop(OWN, 64, resid_rows)
-    swap(3, r.nt.at[pl.ds(0, OWN)], r.nt.at[pl.ds(OWN, OWN)])
-    spread_y("s")
-    spread_z("d")
-    whole("f")
-    whole("s")
-    swapped(3, r.nt.at[pl.ds(OWN, OWN)])
+        r.nt[rows, :] = (v * scale * r.gain[1:2, :]).astype(BF16)
 
     def hidden(at, width):
         a = dot(r.nt[...], r.wf[:, pl.ds(at, width)]).astype(BF16)
@@ -409,109 +431,6 @@
         r.fs[:, pl.ds(FH + at, width)] = b
         r.pr[:, pl.ds(at, width)] = (a.astype(F32) * b.astype(F32)).astype(BF16)
 
-    tile_loop(FH, 256, hidden)
-    loads[1].wait()
-    swapped(1, r.cot.at[pl.ds(OWN, OWN)])
-
-    def chunk_dot(i, cc):
-        kind, at, cols = CHUNKS[i]
-        if kind == "d":
-            out = t_dot(r.pr[...], r.cot[:, lanes_of(512 * cc + at, cols)])
-        elif kind == "f":
-            out = t_dot(r.nt[:, lanes_of(512 * cc, 512)], r.fs[:, pl.ds(at, cols)])
-        elif kind == "o":
-            out = t_dot(r.mix[...], r.bg[:, lanes_of(512 * cc, cols)])
-        else:
-            out = t_dot(r.nrm[:, lanes_of(512 * cc, 512)], r.g4[:, pl.ds(at, cols)])
-        return out.reshape(4, 2, piece_rows(kind), cols)
-
-    buf = lambda name, i: getattr(r, f"{name}{i}")
-    chunk_sends = {}
-
-    def give(i):
-        kind, _, cols = CHUNKS[i]
-        if i >= 4 and i - 2 in chunk_sends:
-            chunk_sends.pop(i - 2).wait_send()
-        stage = r.sbd.at[i % 2] if kind == "d" else r.sbf.at[i % 2, :, :, :, pl.ds(0, cols)]
-        stage[...] = chunk_dot(i, 1 - c).astype(BF16)
-        chunk_sends[i] = send(stage, buf("rb", i), r.r_cs.at[i], r.r_cr.at[i], sib, later=False)
-
-    def take(i):
-        arrived(buf("rb", i), r.r_cr.at[i])
-        own = buf("ow", i)
-        own[...] = (chunk_dot(i, c) + buf("rb", i)[...].astype(F32)).astype(BF16)
-        send(own.at[:, 1 - y], buf("yr", i), r.r_ys.at[i], r.r_yr.at[i], yn)
-
-    def take_y(i):
-        arrived(buf("yr", i), r.r_yr.at[i])
-        own, part = buf("ow", i), buf("yr", i)
-        for k in (1, 3, 2, 0):
-            slot = own.at[zk[k], y]
-            slot[...] = (slot[...].astype(F32) + part[zk[k]].astype(F32)).astype(BF16)
-            if k:
-                send(slot, buf("zr", i).at[3 - k], r.r_zs.at[i, k - 1], r.r_zr.at[i, 3 - k], zp[k])
-
-    finals = []
-
-    def take_z(i):
-        kind, at, cols = CHUNKS[i]
-        own, part, fin = buf("ow", i), buf("zr", i), buf("fin", i)
-        total = own[z, y].astype(F32)
-        for k in range(3):
-            arrived(part.at[k], r.r_zr.at[i, k])
-            total = total + part[k].astype(F32)
-        fin[...] = total
-        if kind in ("f", "a"):
-            if kind == "f":
-                out, place = (r.g1, FH * x + at) if at < FH else (r.g2, FH * x + at - FH)
-            else:
-                out, place = (r.gq, r.gk, r.gv, r.gg)[at // 512], HALF * x
-            dst = out.at[:, lanes_of(place, cols)]
-            finals.append(local(fin.at[rows_of(32 * x, 32, 32)], dst, r.r_fs.at[i, 0]))
-            send(fin.at[rows_of(32 * (1 - x), 32, 32)], dst, r.r_fs.at[i, 1], r.r_fr.at[i, 0], xn)
-            return
-        out = r.gd if kind == "d" else r.go
-        n = 88 if kind == "d" else 32
-        dst = out.at[:, lanes_of(512 * c + at, cols)]
-        for xx in range(2):
-            src = fin.at[pl.ds(n * xx, n)]
-            itself = jnp.logical_and(x == c, x == xx)
-
-            @pl.when(itself)
-            def _():
-                local(src, dst, r.r_fr.at[i, c])
-
-            @pl.when(jnp.logical_not(itself))
-            def _():
-                send(src, dst, r.r_fs.at[i, xx], r.r_fr.at[i, c], dev(x, z, y, xx), later=False)
-
-    def finish(i):
-        kind, at, cols = CHUNKS[i]
-        if kind in ("f", "a"):
-            if kind == "f":
-                out, place = (r.g1, FH * (1 - x) + at) if at < FH else (r.g2, FH * (1 - x) + at - FH)
-            else:
-                out, place = (r.gq, r.gk, r.gv, r.gg)[at // 512], HALF * (1 - x)
-            arrived(out.at[:, lanes_of(place, cols)], r.r_fr.at[i, 0])
-            return
-        out = r.gd if kind == "d" else r.go
-        n = 88 if kind == "d" else 32
-        for cc in range(2):
-            arrived(out.at[:, pl.ds(512 * cc + at, cols)], r.r_fr.at[i, cc])
-        for xx in range(2):
-            itself = jnp.logical_and(x == c, x == xx)
-
-            @pl.when(jnp.logical_not(itself))
-            def _():
-                src = buf("fin", i).at[pl.ds(n * xx, n)]
-                remote(src, src, r.r_fs.at[i, xx], r.r_fs.at[i, xx], xn).wait_send()
-
-    give(0)
-    spread_y("d")
-    give(1)
-    take(0)
-    whole("d")
-
     def hidden_grad(at, width):
         pg = dot_t(r.cot[...], r.wd[pl.ds(at, width), :]).astype(BF16).astype(F32)
         a = r.fs[:, pl.ds(at, width)].astype(F32)
@@ -519,47 +438,29 @@
         r.fs[:, pl.ds(at, width)] = (pg * b).astype(BF16)
         r.fs[:, pl.ds(FH + at, width)] = (pg * a).astype(BF16)
 
-    tile_loop(FH, 256, hidden_grad)
-    tile_loop(D, 256, lambda at, w: split_store(dot_t(r.fs[...], r.wf[pl.ds(at, w), :]), 1, at, w))
-    swap(4, r.es.at[1], r.er.at[1])
-    take(1)
-    give(2)
-    take_y(0)
-    give(3)
-    take(2)
-    swapped(4, r.er.at[1])
-    r.gacc[...] = jnp.zeros((2, 8, D), F32)
-
     def resid_grad_rows(start):
         rows = pl.ds(start, 64)
         ng = r.po[rows, :] + r.er[1, rows, :].astype(F32)
         v = r.res[rows, :]
         scale = lax.rsqrt(jnp.mean(v * v, axis=-1, keepdims=True) + EPS)
-        n = ng * r.gr[12, 1:2, :]
+        n = ng * r.gain[1:2, :]
         grad = r.cot[rows, :].astype(F32) + scale * n - v * (scale * scale * scale * jnp.mean(n * v, axis=-1, keepdims=True))
         r.rg[rows, :] = grad
         r.bg[rows, :] = grad.astype(BF16)
         r.gacc[1] += jnp.sum((ng * v * scale).reshape(8, 8, D), axis=0)
 
-    row_loop(OWN, 64, resid_grad_rows)
-    swap(5, r.bg.at[pl.ds(0, OWN)], r.bg.at[pl.ds(OWN, OWN)])
-    tile_loop(D, 256, lambda at, w: split_store(dot(r.pr[...], r.wd[:, pl.ds(at, w)]), 3, at, w))
-    swap(6, r.es.at[3], r.er.at[3])
-    take_y(1)
-    give(4)
-    take(3)
-    take_z(0)
-    swapped(5, r.bg.at[pl.ds(OWN, OWN)])
-
-    def mixed_grad(at, width):
-        cols = pl.ds(at, width)
-        mg = dot_t(r.bg[...], r.wo[pl.ds(at, width), :]).astype(BF16).astype(F32)
-        g = r.gp[:, cols]
-        s = jax.nn.sigmoid(g)
-        r.dout[:, cols] = (mg * (g * s)).astype(BF16)
-        r.g4[:, pl.ds(3 * HALF + at, width)] = (mg * r.att[:, cols] * (s * (1.0 + g * (1.0 - s)))).astype(BF16)
-
-    tile_loop(HALF, 256, mixed_grad)
+    def mixed_grad(start, count):
+        rows = pl.ds(start, count)
+
+        def tile(at, width):
+            cols = pl.ds(at, width)
+            mg = dot_t(r.bg[rows, :], r.wo[pl.ds(at, width), :]).astype(BF16).astype(F32)
+            g = r.gp[rows, cols]
+            s = jax.nn.sigmoid(g)
+            r.dout[rows, cols] = (mg * (g * s)).astype(BF16)
+            r.g4[rows, pl.ds(3 * HALF + at, width)] = (mg * r.att[rows, cols] * (s * (1.0 + g * (1.0 - s)))).astype(BF16)
+
+        tile_loop(HALF, 256, tile)
 
     def attend_grad(start):
         rows = pl.ds(start, 64)
@@ -578,62 +479,331 @@
             kg = t_dot(sg, q)
             r.g4[rows, pl.ds(HALF + 128 * h, 128)] = (jnp.where(left, kg[:64], kg[64:]) * HDIM ** (-0.5)).astype(BF16)
 
-    row_loop(ROWS, 64, attend_grad)
-    swapped(6, r.er.at[3])
-
     def block_out_rows(start):
         rows = pl.ds(start, 64)
-        r.bo[rows, :] = (r.res[rows, :] + r.po[rows, :] + r.er[3, rows, :].astype(F32)).astype(BF16)
-
-    row_loop(OWN, 64, block_out_rows)
-    outs = [local(r.bo, r.block_out, r.s_out.at[0])]
-    tile_loop(D, 256, lambda at, w: split_store(dot_t(r.g4[...], r.wa[pl.ds(at, w), :]), 2, at, w))
-    swap(7, r.es.at[2], r.er.at[2])
-    take_y(2)
-    give(5)
-    take(4)
-    take_z(1)
-    swapped(7, r.er.at[2])
+        r.bo[rows, :] = (r.res[rows, :] + r.er[0, rows, :].astype(F32)).astype(BF16)
+
+    def block_out_part(at, width):
+        acc = dot(r.pr[...], r.wd[:, pl.ds(at, width)])
+        r.res[:, pl.ds(at, width)] += acc[:OWN]
+        r.es[0, :, pl.ds(at, width)] = acc[OWN:].astype(BF16)
 
     def tokens_grad_rows(start):
         rows = pl.ds(start, 64)
         ng = r.po[rows, :] + r.er[2, rows, :].astype(F32)
         v = r.tok[rows, :].astype(F32)
         scale = lax.rsqrt(jnp.mean(v * v, axis=-1, keepdims=True) + EPS)
-        n = ng * r.gr[12, 0:1, :]
+        n = ng * r.gain[0:1, :]
         r.rg[rows, :] = r.rg[rows, :] + scale * n - v * (scale * scale * scale * jnp.mean(n * v, axis=-1, keepdims=True))
         r.gacc[0] += jnp.sum((ng * v * scale).reshape(8, 8, D), axis=0)
 
-    row_loop(OWN, 64, tokens_grad_rows)
-    outs.append(local(r.rg, r.tokens_grad, r.s_out.at[1]))
-    take_y(3)
-    give(6)
-    take(5)
-    for i in range(7, NCH + 4):
-        if i < NCH:
-            give(i)
-        if i - 1 < NCH:
-            take(i - 1)
-        if 0 <= i - 3 < NCH:
-            take_y(i - 3)
-        if 0 <= i - 5 < NCH:
-            take_z(i - 5)
-        if i == NCH:
+    def chunk_dot(i, cc):
+        kind, at, cols = CHUNKS[i]
+        if kind == "d":
+            out = t_dot(r.pr[...], r.cot[:, lanes_of(512 * cc + at, cols)])
+        elif kind == "f":
+            out = t_dot(r.nt[:, lanes_of(512 * cc, 512)], r.fs[:, pl.ds(at, cols)])
+        elif kind == "o":
+            out = t_dot(r.mix[...], r.bg[:, lanes_of(512 * cc, cols)])
+        else:
+            out = t_dot(r.nrm[:, lanes_of(512 * cc, 512)], r.g4[:, pl.ds(at, cols)])
+        return out.reshape(4, 2, piece_rows(kind), cols)
+
+    buf = lambda name, i: getattr(r, f"{name}{i}")
+    chunk_sends = {}
+
+    def give(i):
+        kind, _, cols = CHUNKS[i]
+        if i >= 4 and i - 2 in chunk_sends:
+            chunk_sends.pop(i - 2).wait_send()
+        stage = r.sbd.at[i % 2] if kind == "d" else r.sbf.at[i % 2, :, :, :, pl.ds(0, cols)]
+        stage[...] = chunk_dot(i, 1 - c).astype(BF16)
+        chunk_sends[i] = send(stage, buf("rb", i), r.r_cs.at[i], r.r_cr.at[i], sib, later=False)
+
+    def take(i):
+        arrived(buf("rb", i), r.r_cr.at[i])
+        own = buf("ow", i)
+        own[...] = (chunk_dot(i, c) + buf("rb", i)[...].astype(F32)).astype(BF16)
+        if Z_FIRST[i]:
+            to_owners(i)
+        else:
+            send(own.at[:, 1 - y], buf("yr", i), r.r_ys.at[i], r.r_yr.at[i], yn)
+
+    def z_slot(i, zz):
+        own = buf("ow", i)
+        return own.at[zz] if Z_FIRST[i] else own.at[zz, y]
+
+    def to_owners(i):
+        beside = dev(c, jnp.where(z == 3, 2, 1), y, x)
+        far = jnp.where(z == 3, 0, 3)
+        send_if(jnp.logical_not(inner), z_slot(i, far), buf("zx", i), r.r_zs.at[i, 2], r.r_zx.at[i], beside)
+        for k in (1, 3):
+            slot = z_slot(i, zk[k])
+            send_if(z != (3 if k == 1 else 0), slot, buf("zr", i).at[3 - k], r.r_zs.at[i, 1 if k == 3 else 0], r.r_zr.at[i, 3 - k], zp[k])
+        two = z_slot(i, zk[2])
+        send_if(jnp.logical_not(inner), two, buf("zr", i).at[1], r.r_zt.at[i], r.r_zr.at[i, 1], zp[2])
+
+    def pass_far(i):
+        two = z_slot(i, zk[2])
+
+        @pl.when(inner)
+        def _():
+            arrived(buf("zx", i), r.r_zx.at[i])
+            two[...] = (two[...].astype(F32) + buf("zx", i)[...].astype(F32)).astype(BF16)
+
+        send_if(inner, two, buf("zr", i).at[1], r.r_zs.at[i, 2], r.r_zr.at[i, 1], zp[2])
+
+    def take_y(i):
+        own, part = buf("ow", i), buf("yr", i)
+        arrived(part, r.r_yr.at[i])
+        if Z_FIRST[i]:
+            return
+        for k in range(4):
+            slot = own.at[zk[k], y]
+            slot[...] = (slot[...].astype(F32) + part[zk[k]].astype(F32)).astype(BF16)
+        to_owners(i)
+
+    finals = []
+
+    def add_z(i, dst, first, half=None):
+        part = buf("zr", i)
+        take_part = (lambda j: part[j]) if half is None else (lambda j: part[j, half])
+        if not half:
+            arrived(part.at[1], r.r_zr.at[i, 1])
+        dst[...] = first + take_part(1).astype(F32)
+        for j, end in ((0, 3), (2, 0)):
+
+            @pl.when(z != end)
+            def _():
+                if not half:
+                    arrived(part.at[j], r.r_zr.at[i, j])
+                dst[...] += take_part(j).astype(F32)
+
+    def owner_sum(i):
+        own, fin = buf("ow", i), buf("fin", i)
+        for half in range(2):
+            add_z(i, fin, own[z, half].astype(F32), half)
+            own[z, half] = fin[...].astype(BF16)
+        send(own.at[z, 1 - y], buf("yr", i), r.r_ys.at[i], r.r_yr.at[i], yn)
+
+    def take_z(i):
+        kind, at, cols = CHUNKS[i]
+        own, fin = buf("ow", i), buf("fin", i)
+        if Z_FIRST[i]:
+            fin[...] = own[z, y].astype(F32) + buf("yr", i)[...].astype(F32)
+        else:
+            add_z(i, fin, own[z, y].astype(F32))
+        if kind in ("f", "a"):
+            if kind == "f":
+                out, place = (r.g1, FH * x + at) if at < FH else (r.g2, FH * x + at - FH)
+            else:
+                out, place = (r.gq, r.gk, r.gv, r.gg)[at // 512], HALF * x
+            dst = out.at[:, lanes_of(place, cols)]
+            finals.append(local(fin.at[rows_of(32 * x, 32, 32)], dst, r.r_fs.at[i, 0]))
+            send(fin.at[rows_of(32 * (1 - x), 32, 32)], dst, r.r_fs.at[i, 1], r.r_fr.at[i, 0], xn)
+            return
+        out = r.gd if kind == "d" else r.go
+        n = 88 if kind == "d" else 32
+        dst = out.at[:, lanes_of(512 * c + at, cols)]
+        for xx in range(2):
+            src = fin.at[pl.ds(n * xx, n)]
+            itself = jnp.logical_and(x == c, x == xx)
+
+            @pl.when(itself)
+            def _():
+                local(src, dst, r.r_fr.at[i, c])
+
+            @pl.when(jnp.logical_not(itself))
+            def _():
+                send(src, dst, r.r_fs.at[i, xx], r.r_fr.at[i, c], dev(x, z, y, xx), later=False)
+
+    def finish(i):
+        kind, at, cols = CHUNKS[i]
+        if kind in ("f", "a"):
+            if kind == "f":
+                out, place = (r.g1, FH * (1 - x) + at) if at < FH else (r.g2, FH * (1 - x) + at - FH)
+            else:
+                out, place = (r.gq, r.gk, r.gv, r.gg)[at // 512], HALF * (1 - x)
+            arrived(out.at[:, lanes_of(place, cols)], r.r_fr.at[i, 0])
+            return
+        out = r.gd if kind == "d" else r.go
+        n = 88 if kind == "d" else 32
+        for cc in range(2):
+            arrived(out.at[:, pl.ds(512 * cc + at, cols)], r.r_fr.at[i, cc])
+        for xx in range(2):
+            itself = jnp.logical_and(x == c, x == xx)
+
+            @pl.when(jnp.logical_not(itself))
+            def _():
+                src = buf("fin", i).at[pl.ds(n * xx, n)]
+                remote(src, src, r.r_fs.at[i, xx], r.r_fs.at[i, xx], xn).wait_send()
+
+    def over(start, count, fn):
+        row_loop(count, 64, lambda at: fn(at + start))
+
+    def swap_rows(i, src, dst, start, count):
+        swap(i, src.at[pl.ds(start, count)], dst.at[pl.ds(start, count)])
+
+    def swapped_rows(i, dst, start, count):
+        swapped(i, dst.at[pl.ds(start, count)])
+
+    load_tok = local(r.tokens, r.tok.at[pl.ds(0, OWN)], r.s_loc.at[0])
+    load_cot = local(r.cot_in, r.cot.at[pl.ds(0, OWN)], r.s_loc.at[1])
+    outs = []
+
+    def do_start():
+        start_cols("a")
+        start_cols("b")
+        r.gacc[...] = jnp.zeros((2, 8, D), F32)
+
+    def do_start2():
+        start_rows("o")
+        start_cols("s")
+        start_cols("f")
+        start_rows("d")
+        swap(0, r.tokens, r.tok.at[pl.ds(OWN, OWN)])
+        swap(1, r.cot_in, r.cot.at[pl.ds(OWN, OWN)])
+
+    def do_norm_own():
+        load_tok.wait()
+        over(0, OWN, lambda start: norm_rows(start, 0, r.po))
+
+    def do_norm_partner():
+        swapped(0, r.tok.at[pl.ds(OWN, OWN)])
+        over(0, OWN, lambda start: norm_rows(start, OWN, r.rg))
+
+    def do_proj():
+        unit_row = lax.broadcasted_iota(jnp.int32, (8, 128), 0)
+        unit = jnp.where(unit_row == lax.broadcasted_iota(jnp.int32, (8, 128), 1), 1.0, 0.0).astype(BF16)
+        r.gain[...] = dot_t(unit, r.wa[:, pl.ds(4 * HALF, 128)])
+        row_loop(OWN, 64, gain_rows)
+        tile_loop(3 * HALF, 256, proj)
+        tile_loop(HALF, 256, proj_gate)
+
+    def do_out(start):
+        if start == 0:
+            partial_rows(r.mix, out_product, 0, 0, 256)
+            return
+        partial_rows(r.mix, out_product, 0, start, 128)
+        swap_rows(2 if start == 256 else 3, r.es.at[0], r.er.at[0], start - OWN, 128)
+
+    def do_resid(start):
+        swapped_rows(2 + start // 128, r.er.at[0], start, 128)
+        over(start, 128, resid_rows)
+        swap(4 + start // 128, r.nt.at[pl.ds(start, 128)], r.nt.at[pl.ds(OWN + start, 128)])
+
+    def do_hidden():
+        swapped(4, r.nt.at[pl.ds(OWN, 128)])
+        swapped(5, r.nt.at[pl.ds(OWN + 128, 128)])
+        tile_loop(FH, 256, hidden)
+
+    def do_cot():
+        load_cot.wait()
+        swapped(1, r.cot.at[pl.ds(OWN, OWN)])
+
+    def do_back(start):
+        if start == 0:
+            partial_rows(r.fs, hidden_back, 1, 0, 256)
+            return
+        partial_rows(r.fs, hidden_back, 1, start, 128)
+        swap_rows(6 if start == 256 else 7, r.es.at[1], r.er.at[1], start - OWN, 128)
+
+    def do_resid_grad(start):
+        swapped_rows(6 + start // 128, r.er.at[1], start, 128)
+        over(start, 128, resid_grad_rows)
+        swap(8 + start // 128, r.bg.at[pl.ds(start, 128)], r.bg.at[pl.ds(OWN + start, 128)])
+
+    def do_mixed_grad(start):
+        if start == 0:
+            mixed_grad(0, 256)
+            return
+        swapped(8 if start == 256 else 9, r.bg.at[pl.ds(start, 128)])
+        mixed_grad(start, 128)
+
+    def do_heads_back(start):
+        partial_rows(r.g4, heads_back, 2, start, 256)
+        if start:
+            swap(11, r.es.at[2], r.er.at[2])
+
+    def do_block_out():
+        swaps.pop(2).wait_send()
+        swaps.pop(3).wait_send()
+        tile_loop(D, 256, block_out_part)
+        swap(10, r.es.at[0], r.er.at[0])
+
+    def do_tokens_grad():
+        swapped(11, r.er.at[2])
+        over(0, OWN, tokens_grad_rows)
+        outs.append(local(r.rg, r.tokens_grad, r.s_out.at[1]))
+
+    def do_block_rows():
+        swapped(10, r.er.at[0])
+        over(0, OWN, block_out_rows)
+        outs.append(local(r.bo, r.block_out, r.s_out.at[0]))
+
+    def do_gsum(n):
+        if n == 0:
             which = lax.broadcasted_iota(jnp.int32, (8, D), 0)
-            a = jnp.sum(r.gacc[0], axis=0, keepdims=True)
-            b = jnp.sum(r.gacc[1], axis=0, keepdims=True)
             zero = jnp.zeros((8, D), F32)
-            total = sum_small(1, jnp.where(which == 0, a, zero) + jnp.where(which == 1, b, zero))
-            r.gacc[0] = total
+            sums = [jnp.sum(r.gacc[i], axis=0, keepdims=True) for i in range(2)]
+            grad_sum(0, jnp.where(which == 0, sums[0], zero) + jnp.where(which == 1, sums[1], zero))
+        elif n < 4:
+            grad_sum(n)
+        else:
+            r.gacc[0] = grad_sum(4)
             outs.append(local(r.gacc.at[0], r.gain_grads, r.s_out.at[2]))
-    take_z(NCH - 1)
-    for i in range(NCH):
-        finish(i)
-    for copy in list(chunk_sends.values()) + sends:
+
+    def do_take_z(i):
+        if Z_FIRST[i]:
+            take_y(i)
+        take_z(i)
+
+    def do_attend(start):
+        over(start, 64, attend)
+
+    def do_hidden_grad():
+        tile_loop(FH, 256, hidden_grad)
+
+    def do_attend_grad(start):
+        over(start, 64, attend_grad)
+
+    work = (
+        (do_start,), (own, GA), (own, GB), (do_start2,), (got_y, GA, 0), (own, GO), (got_z, GA, 1, 0),
+        (got_z, GA, 2, 0), (got_y, GB, 0), (got_z, GO, 1, 0), (got_z, GB, 1, 0), (got_z, GO, 2, 0), (do_norm_own,),
+        (got_z, GO, 3, 0), (got_z, GB, 2, 0), (got_z, GA, 3, 0), (got_z, GB, 3, 0), (got_y, GO, 1), (got_y, GO, 0),
+        (got_y, GO, 3), (own, GF), (do_norm_partner,), (got_y, GB, 2), (got_y, GA, 1), (got_y, GB, 1), (own, GD),
+        (own, GS), (got_z, GF, 1, 0), (got_y, GA, 3), (got_y, GA, 2), (got_y, GO, 2), (got_y, GB, 3), (whole, GB),
+        (whole, GA), (do_proj,), (got_z, GS, 1, 0), (do_attend, 0), (do_attend, 320), (got_y, GD, 0),
+        (do_attend, 256), (whole, GO), (got_z, GS, 2, 0), (do_attend, 448), (do_out, 256), (do_attend, 384),
+        (got_y, GF, 0), (got_z, GF, 2, 0), (got_z, GD, 1, 0), (do_attend, 64), (do_attend, 192), (got_z, GD, 2, 0),
+        (got_y, GS, 0), (got_y, GF, 1), (do_out, 384), (got_z, GS, 3, 0), (got_z, GD, 1, 1), (got_y, GS, 1),
+        (do_attend, 128), (got_y, GS, 2), (do_out, 0), (do_resid, 0), (got_z, GF, 3, 0), (do_resid, 128),
+        (got_y, GF, 2), (got_z, GD, 3, 0), (got_z, GD, 2, 1), (got_y, GS, 3), (got_y, GF, 3), (whole, GS),
+        (got_z, GD, 3, 1), (whole, GF), (do_hidden,), (do_cot,), (give, 0), (give, 1), (whole, GD), (do_hidden_grad,),
+        (take, 0), (do_back, 256), (take, 1), (give, 2), (do_back, 384), (take, 2), (do_back, 0), (give, 3),
+        (do_resid_grad, 0), (pass_far, 1), (give, 4), (take_y, 0), (do_resid_grad, 128), (take, 3),
+        (do_mixed_grad, 0), (owner_sum, 1), (do_attend_grad, 0), (take_y, 2), (pass_far, 0), (do_attend_grad, 64),
+        (give, 5), (take, 4), (do_attend_grad, 192), (do_attend_grad, 128), (do_mixed_grad, 256),
+        (do_mixed_grad, 384), (give, 6), (take_y, 3), (pass_far, 2), (do_attend_grad, 448), (take, 5), (give, 7),
+        (do_attend_grad, 256), (do_take_z, 0), (do_attend_grad, 384), (take, 7), (do_attend_grad, 320),
+        (do_heads_back, 256), (pass_far, 3), (do_take_z, 1), (pass_far, 7), (do_heads_back, 0), (take, 6),
+        (take_y, 4), (give, 8), (do_block_out,), (take_y, 5), (take, 8), (give, 9), (give, 10), (pass_far, 4),
+        (do_tokens_grad,), (do_gsum, 0), (take, 9), (do_take_z, 2), (owner_sum, 7), (take_y, 6), (take_y, 8),
+        (pass_far, 5), (do_take_z, 4), (do_take_z, 3), (finish, 0), (take, 10), (pass_far, 8), (do_gsum, 1),
+        (pass_far, 6), (take_y, 9), (pass_far, 9), (finish, 2), (do_take_z, 6), (do_take_z, 7), (do_take_z, 5),
+        (take_y, 10), (finish, 1), (finish, 4), (pass_far, 10), (do_take_z, 9), (do_gsum, 2), (finish, 6),
+        (do_take_z, 8), (do_gsum, 3), (do_take_z, 10), (finish, 7), (finish, 8), (finish, 5), (finish, 3),
+        (finish, 9), (do_block_rows,), (finish, 10), (do_gsum, 4),
+    )
+    for step, *args in work:
+        step(*args)
+    for copy in list(chunk_sends.values()) + list(swaps.values()) + sends:
         copy.wait_send()
+    for pred, copy in guarded:
+        pl.when(pred)(copy.wait_send)
     for copy in finals + outs:
         copy.wait()
-    for g in ("a", "f", "s"):
+    for g in "abfs":
         gi = GROUPS.index(g)
         own = col_shard(g, x)
         remote(own, own, r.s_xs.at[gi, 0], r.s_xs.at[gi, 0], xn).wait_send()
@@ -648,15 +818,30 @@
         remote(block, block, r.s_xs.at[gi, 1], r.s_xs.at[gi, 1], xn).wait_send()
 
 
+def hand_over(gain_ref, *refs):
+    count = (len(refs) - 4) // 3
+    ins, (one, two), outs = refs[:count], refs[count : count + 2], refs[count + 2 : 2 * count + 2]
+    held, (in_sems, out_sems) = refs[2 * count + 2 : -2], refs[-2:]
+    loads = [pltpu.make_async_copy(a, b, in_sems.at[i]) for i, (a, b) in enumerate(zip(ins, held))]
+    stores = [pltpu.make_async_copy(a, b, out_sems.at[i]) for i, (a, b) in enumerate(zip(held, outs))]
+    for load in loads:
+        load.start()
+    me = lax.axis_index("dp") * 16 + lax.axis_index("fsdp")
+    block = gain_ref[:, lanes_of(128 * (me // 4), 128)]
+    block = pltpu.roll(block, lax.rem(128 - 32 * lax.rem(me, 4), 128), 1)
+    one[...] = block[0, :32]
+    two[...] = block[1, :32]
+    for load, store in zip(loads, stores):
+        load.wait()
+        store.start()
+    for store in stores:
+        store.wait()
+
+
 def fused_layer(
     tokens, attn_gain, w_query, w_key, w_value, w_gate, w_output, ffn_gain, w_first, w_second, w_down, cotangent
 ):
-    me = lax.axis_index("dp") * 16 + lax.axis_index("fsdp")
-    lane = lax.broadcasted_iota(jnp.int32, (8, D), 1)
-    row = lax.broadcasted_iota(jnp.int32, (8, D), 0)
-    mine = lane // 32 == me
-    spread = lambda gain: jnp.tile(gain.astype(F32), 32)[None, :]
-    gains = jnp.where(mine & (row == 0), spread(attn_gain), 0.0) + jnp.where(mine & (row == 1), spread(ffn_gain), 0.0)
+    gains = jnp.pad(jnp.stack([attn_gain, ffn_gain], axis=1), ((0, 0), (0, 126)))
     items = scratch_list()
     names = IN_NAMES + OUT_NAMES + tuple(name for name, _ in items)
     shape = jax.ShapeDtypeStruct
@@ -674,8 +859,20 @@
         name="layer",
     )(tokens, gains, w_query, w_key, w_value, w_gate, w_output, w_first, w_second, w_down, cotangent)
     block_out, tokens_grad, gain_grads, gq, gk, gv, gg, go, g1, g2, gd = outs
-    own = lax.dynamic_slice(gain_grads, (0, me * 32), (8, 32))
-    return block_out, tokens_grad, own[0], gq, gk, gv, gg, go, own[1], g1, g2, gd
+    kept = (block_out, tokens_grad, gq, gk, gv, gg, go, g1, g2, gd)
+    anywhere = pl.BlockSpec(memory_space=pl.ANY)
+    in_vmem = pl.BlockSpec(memory_space=pltpu.VMEM)
+    gain_one, gain_two, *rest = pl.pallas_call(
+        hand_over,
+        out_shape=[shape((32,), F32)] * 2 + [shape(v.shape, v.dtype) for v in kept],
+        in_specs=[in_vmem] + [anywhere] * len(kept),
+        out_specs=[in_vmem] * 2 + [anywhere] * len(kept),
+        scratch_shapes=[pltpu.VMEM(v.shape, v.dtype) for v in kept] + [pltpu.SemaphoreType.DMA((len(kept),))] * 2,
+        compiler_params=pltpu.CompilerParams(vmem_limit_bytes=63 * 2**20),
+        name="hand_over",
+    )(gain_grads, *kept)
+    block_out, tokens_grad, gq, gk, gv, gg, go, g1, g2, gd = rest
+    return block_out, tokens_grad, gain_one, gq, gk, gv, gg, go, gain_two, g1, g2, gd
 
 
 def rms_scale(values, gain):

time: 266 us -> 181 us (0.68)
  Pallas kernels: 251 us -> 178 us
  local copies, waits for them, and re-layouts: 12.8 us -> 1.37 us
    pallas_call x1, Pallas kernels: 251 us -> 174 us  [fused_layer(): pl.pallas_call(functools.partial(layer_kernel, names), out_shape=[shape((...]
    unnamed x32 -> x4, local copies, waits for them, and re-layouts: 11.3 us -> 0.66 us
    pallas_call x0 -> x1, Pallas kernels: none -> 4.38 us  [fused_layer(): pl.pallas_call(hand_over, out_shape=[shape((32,), F32)] * 2 + [shape(v.sh...]
where the time goes in v3:
time: 181 us
  Pallas kernels  178 us (98%)
    pallas_call x1, Pallas kernels, fused_layer(): pl.pallas_call(functools.partial(layer_kernel, names), out_shape=[shape((...  174 us
    pallas_call x1, Pallas kernels, fused_layer(): pl.pallas_call(hand_over, out_shape=[shape((32,), F32)] * 2 + [shape(v.sh...  4.38 us

profile of v3, /device:TPU:0, one launch (start us, length us, event | category | flops | bytes accessed | tf_op | source)
XLA Modules:
  0.0 180.6 jit_solution(7646116825369817060)
XLA Ops:
  0.6 0.0 copy-start
  0.7 0.0 copy-start.1
  0.7 0.6 copy-done
  1.3 0.0 copy-done.1
  1.3 0.1 copy.26
  1.4 0.6 pad.4.refs_1_
  2.0 174.0 %layer.1 = (bf16[256,1024]{1,0:T(8,128)(2,1)}, f32[256,1024]{1,0:T(8,128)}, f32[8,1024]{1,0:T(8,128)}, f32[32,1024]{1,0:T(8,128)}, f32[32,1024]{1,0:T(8,128)}, /...) custom-call(bf16[256,1024]{1,0:T(8,128)(2,1)} %refs_0_.1, ...), custom_call_target="tpu_custom_call" | custom-call | tf_op jit(solution)/shard_map/layer/pallas_call | solution.py:848
  176.0 4.4 %hand_over.1 = (f32[32]{0:T(128)}, f32[32]{0:T(128)}, bf16[256,1024]{1,0:T(8,128)(2,1)}, f32[256,1024]{1,0:T(8,128)}, f32[32,1024]{1,0:T(8,128)}, /*index=5*/f32...) custom-call(f32[8,1024]{1,0:T(8,128)} %get-tuple-element.35.gain_ref, ...), custom_call_target="tpu_custom_call" | custom-call | tf_op jit(solution)/shard_map/hand_over/pallas_call | solution.py:865
  (1 shorter events, 0.0 us)
Async XLA Ops:
  0.6 0.7 copy-start
  0.7 0.7 copy-start.1

commit v4 on v3

--- a/solution.py
+++ b/solution.py
@@ -32,9 +32,10 @@
 )
 NCH = len(CHUNKS)
 Z_FIRST = tuple(i in (1, 7,) for i in range(NCH))
-Y_FIRST = ("d",)
-GROUPS = ("a", "b", "o", "f", "s", "d")
-GA, GB, GO, GF, GS, GD = GROUPS
+Y_FIRST = ("s",)
+GROUPS = ("a", "b", "o", "f", "s", "g", "t", "d")
+GA, GB, GO, GF, GS, GG, GT, GD = GROUPS
+SPANS = {"a": (0, 1152), "b": (1152, 1024), "f": (0, 768), "g": (768, 640), "s": (FH, 768), "t": (FH + 768, 640)}
 
 
 def piece_rows(kind):
@@ -53,7 +54,7 @@
         ("pr", vm((ROWS, FH), BF16)), ("g4", vm((ROWS, 4 * HALF), BF16)), ("bg", vm((ROWS, D), BF16)),
         ("rg", vm((OWN, D), F32)), ("po", vm((OWN, D), F32)), ("bo", vm((OWN, D), BF16)),
         ("es", vm((3, OWN, D), BF16)), ("er", vm((3, OWN, D), BF16)),
-        ("gs", vm((4, 8, D), F32)), ("gr", vm((6, 8, D), F32)), ("gain", vm((8, D), F32)), ("gacc", vm((2, 8, D), F32)),
+        ("gs", vm((4, 8, D), F32)), ("gr", vm((6, 8, D), F32)), ("gain", vm((8, D), F32)), ("gains", vm((32, 128), BF16)), ("gacc", vm((2, 8, D), F32)),
         ("sbd", vm((2, 4, 2, 176, 256), BF16)), ("sbf", vm((2, 4, 2, 64, 768), BF16)),
     ]
     for i, (kind, _, cols) in enumerate(CHUNKS):
@@ -79,7 +80,7 @@
     return items
 
 
-IN_NAMES = ("tokens", "gains", "wq", "wk", "wv", "wg", "wo_in", "w1", "w2", "wd_in", "cot_in")
+IN_NAMES = ("tokens", "gain_a", "gain_f", "wq", "wk", "wv", "wg", "wo_in", "w1", "w2", "wd_in", "cot_in")
 OUT_NAMES = ("block_out", "tokens_grad", "gain_grads", "gq", "gk", "gv", "gg", "go", "g1", "g2", "gd")
 
 
@@ -173,40 +174,36 @@
     m = z * 2 + y
 
     def piece(g, cc, zz, yy):
-        if g in "ab":
-            cols = pl.ds(0, 1024) if g == "a" else pl.ds(1024, 1024 + 128)
-            return r.wa.at[rows_of(64 * (cc * 8 + zz * 2 + yy), 64, 64), cols]
-        if g == "f":
-            return r.wf.at[rows_of(64 * (cc * 8 + zz * 2 + yy), 64, 64), pl.ds(0, FH)]
-        if g == "s":
-            return r.wf.at[rows_of(64 * (cc * 8 + zz * 2 + yy), 64, 64), pl.ds(FH, FH)]
+        if g in SPANS:
+            full = r.wa if g in "ab" else r.wf
+            return full.at[rows_of(64 * (cc * 8 + zz * 2 + yy), 64, 64), pl.ds(*SPANS[g])]
         if g == "o":
             return r.wo.at[rows_of(64 * (zz * 2 + yy), 64, 64), lanes_of(512 * cc, 512)]
         return r.wd.at[rows_of(176 * (zz * 2 + yy), 176, 16), lanes_of(512 * cc, 512)]
 
     def col_shard(g, who):
         row = rows_of(64 * p + 32 * who, 32, 32)
-        if g in "ab":
-            return r.wa.at[row, pl.ds(0, 1024) if g == "a" else pl.ds(1024, 1024 + 128)]
-        return r.wf.at[row, pl.ds(0 if g == "f" else FH, FH)]
+        return (r.wa if g in "ab" else r.wf).at[row, pl.ds(*SPANS[g])]
 
     def start_cols(g):
         gi = GROUPS.index(g)
-        if g in "ab":
-            first = 0 if g == "a" else 2
-            parts = [(w, HALF, HALF * j) for j, w in enumerate((r.wq, r.wk, r.wv, r.wg))][first : first + 2]
-            full = r.wa
+        if g == "a":
+            parts = [(r.wq, HALF, 0, HALF, 0), (r.wk, HALF, 0, HALF, HALF)]
+        elif g == "b":
+            parts = [(r.wv, HALF, 0, HALF, 1152), (r.wg, HALF, 0, HALF, 1152 + HALF)]
         else:
-            parts = [(r.w1, FH, 0)] if g == "f" else [(r.w2, FH, FH)]
-            full = r.wf
+            at, cols = SPANS[g]
+            parts = [(r.w1 if g in "fg" else r.w2, FH, at % FH, cols, at)]
+        full = r.wa if g in "ab" else r.wf
         row = rows_of(64 * p + 32 * x, 32, 32)
-        if g == "b":
-            local(r.gains, full.at[row, pl.ds(4 * HALF, 128)], r.s_wl.at[gi])
-            send(r.gains, full.at[row, pl.ds(4 * HALF, 128)], r.s_xs.at[gi, 0], r.s_xr.at[gi], xn, later=False)
-        for w, width, at in parts:
-            local(w.at[:, lanes_of(width * x, width)], full.at[row, pl.ds(at, width)], r.s_wl.at[gi])
+        if g == "a":
+            local(r.gains, full.at[row, pl.ds(1024, 128)], r.s_wl.at[gi])
+            send(r.gains, full.at[row, pl.ds(1024, 128)], r.s_xs.at[gi, 0], r.s_xr.at[gi], xn, later=False)
+        for w, half, first, cols, at in parts:
+            dst = full.at[row, pl.ds(at, cols)]
+            local(w.at[:, lanes_of(half * x + first, cols)], dst, r.s_wl.at[gi])
             send(
-                w.at[:, lanes_of(width * (1 - x), width)], full.at[row, pl.ds(at, width)],
+                w.at[:, lanes_of(half * (1 - x) + first, cols)], dst,
                 r.s_xs.at[gi, 0], r.s_xr.at[gi], xn, later=False,
             )
 
@@ -234,7 +231,7 @@
 
     def piece_ready(g):
         gi = GROUPS.index(g)
-        if g in "abfs":
+        if g in SPANS:
             own = col_shard(g, x)
             pltpu.make_async_copy(own, own, r.s_wl.at[gi]).wait()
             arrived(col_shard(g, 1 - x), r.s_xr.at[gi])
@@ -353,11 +350,11 @@
         r.nrm[rows, :] = (r.po[rows, :] * r.gain[0:1, :]).astype(BF16)
         r.nrm[pl.ds(start + OWN, 64), :] = (r.rg[rows, :] * r.gain[0:1, :]).astype(BF16)
 
-    def proj(at, width):
-        r.qkv[:, pl.ds(at, width)] = dot(r.nrm[...], r.wa[:, pl.ds(at, width)]).astype(BF16)
+    def proj(at, width, shift=0):
+        r.qkv[:, pl.ds(at + shift, width)] = dot(r.nrm[...], r.wa[:, pl.ds(at + shift + shift // 8, width)]).astype(BF16)
 
     def proj_gate(at, width):
-        r.gp[:, pl.ds(at, width)] = dot(r.nrm[...], r.wa[:, pl.ds(3 * HALF + at, width)])
+        r.gp[:, pl.ds(at, width)] = dot(r.nrm[...], r.wa[:, pl.ds(1152 + HALF + at, width)])
 
     lane = lax.broadcasted_iota(jnp.int32, (64, 128), 1)
     row = lax.broadcasted_iota(jnp.int32, (64, 128), 0)
@@ -380,21 +377,24 @@
         b = jnp.max(jnp.where(left, low, v), axis=-1, keepdims=True)
         return jnp.where(left, a, b)
 
+    def head_cols(base, h):
+        return pl.ds(base + 128 * h, 128)
+
     def attend(start):
-        rows = pl.ds(start, 64)
-        for h in range(4):
-            cols = pl.ds(128 * h, 128)
-            q = r.qkv[rows, cols]
-            k = r.qkv[rows, pl.ds(HALF + 128 * h, 128)]
-            v = r.qkv[rows, pl.ds(2 * HALF + 128 * h, 128)]
-            s = jnp.where(causal, dot_t(q, pair(k)) * HDIM ** (-0.5), -1e30)
-            e = jnp.exp(s - half_max(s))
-            prob = e / half_sum(e)
-            r.prob[rows, cols] = prob
-            att = dot(prob.astype(BF16), pair(v))
-            r.att[rows, cols] = att
-            g = r.gp[rows, cols]
-            r.mix[rows, cols] = (att * (g * jax.nn.sigmoid(g))).astype(BF16)
+        rows, heads = pl.ds(start, 64), range(4)
+        q = [r.qkv[rows, head_cols(0, h)] for h in heads]
+        k = [r.qkv[rows, head_cols(HALF, h)] for h in heads]
+        v = [r.qkv[rows, head_cols(2 * HALF, h)] for h in heads]
+        g = [r.gp[rows, head_cols(0, h)] for h in heads]
+        s = [jnp.where(causal, dot_t(a, pair(b)) * HDIM ** (-0.5), -1e30) for a, b in zip(q, k)]
+        e = [jnp.exp(a - half_max(a)) for a in s]
+        prob = [a / half_sum(a) for a in e]
+        att = [dot(a.astype(BF16), pair(b)) for a, b in zip(prob, v)]
+        mix = [(a * (b * jax.nn.sigmoid(b))).astype(BF16) for a, b in zip(att, g)]
+        for h in heads:
+            r.prob[rows, head_cols(0, h)] = prob[h]
+            r.att[rows, head_cols(0, h)] = att[h]
+            r.mix[rows, head_cols(0, h)] = mix[h]
 
     def partial_rows(left, right, slot, start, count):
         rows = pl.ds(start, count)
@@ -415,7 +415,8 @@
         return dot_t(v, r.wf[pl.ds(at, width), :])
 
     def heads_back(v, at, width):
-        return dot_t(v, r.wa[pl.ds(at, width), pl.ds(0, 4 * HALF)])
+        left, right = v[:, : 2 * HALF], v[:, 2 * HALF :]
+        return dot_t(left, r.wa[pl.ds(at, width), pl.ds(0, 1024)]) + dot_t(right, r.wa[pl.ds(at, width), pl.ds(1152, 1024)])
 
     def resid_rows(start):
         rows = pl.ds(start, 64)
@@ -463,21 +464,21 @@
         tile_loop(HALF, 256, tile)
 
     def attend_grad(start):
-        rows = pl.ds(start, 64)
-        for h in range(4):
-            cols = pl.ds(128 * h, 128)
-            q = r.qkv[rows, cols]
-            k = r.qkv[rows, pl.ds(HALF + 128 * h, 128)]
-            v = r.qkv[rows, pl.ds(2 * HALF + 128 * h, 128)]
-            do = r.dout[rows, cols]
-            prob = r.prob[rows, cols]
-            vg = t_dot(prob.astype(BF16), do)
-            r.g4[rows, pl.ds(2 * HALF + 128 * h, 128)] = jnp.where(left, vg[:64], vg[64:]).astype(BF16)
-            pg = dot_t(do, pair(v))
-            sg = (prob * (pg - half_sum(prob * pg))).astype(BF16)
-            r.g4[rows, cols] = (dot(sg, pair(k)) * HDIM ** (-0.5)).astype(BF16)
-            kg = t_dot(sg, q)
-            r.g4[rows, pl.ds(HALF + 128 * h, 128)] = (jnp.where(left, kg[:64], kg[64:]) * HDIM ** (-0.5)).astype(BF16)
+        rows, heads = pl.ds(start, 64), range(4)
+        q = [r.qkv[rows, head_cols(0, h)] for h in heads]
+        k = [r.qkv[rows, head_cols(HALF, h)] for h in heads]
+        v = [r.qkv[rows, head_cols(2 * HALF, h)] for h in heads]
+        do = [r.dout[rows, head_cols(0, h)] for h in heads]
+        prob = [r.prob[rows, head_cols(0, h)] for h in heads]
+        pg = [dot_t(a, pair(b)) for a, b in zip(do, v)]
+        vg = [t_dot(a.astype(BF16), b) for a, b in zip(prob, do)]
+        sg = [(a * (b - half_sum(a * b))).astype(BF16) for a, b in zip(prob, pg)]
+        qg = [dot(a, pair(b)) * HDIM ** (-0.5) for a, b in zip(sg, k)]
+        kg = [t_dot(a, b) for a, b in zip(sg, q)]
+        for h in heads:
+            r.g4[rows, head_cols(0, h)] = qg[h].astype(BF16)
+            r.g4[rows, head_cols(HALF, h)] = (jnp.where(left, kg[h][:64], kg[h][64:]) * HDIM ** (-0.5)).astype(BF16)
+            r.g4[rows, head_cols(2 * HALF, h)] = jnp.where(left, vg[h][:64], vg[h][64:]).astype(BF16)
 
     def block_out_rows(start):
         rows = pl.ds(start, 64)
@@ -652,14 +653,22 @@
     outs = []
 
     def do_start():
+        eye = lax.broadcasted_iota(jnp.int32, (32, 32), 0) == lax.broadcasted_iota(jnp.int32, (32, 32), 1)
+        column = lax.broadcasted_iota(jnp.int32, (32, 128), 1)
+        total = jnp.zeros((32, 128), F32)
+        for i, ref in enumerate((r.gain_a, r.gain_f)):
+            values = jnp.broadcast_to(ref[...].astype(F32)[None, :], (32, 32))
+            upright = jnp.sum(jnp.where(eye, values, 0.0), axis=1, keepdims=True)
+            total = total + jnp.where(column == i, upright, 0.0)
+        r.gains[...] = total.astype(BF16)
         start_cols("a")
         start_cols("b")
         r.gacc[...] = jnp.zeros((2, 8, D), F32)
 
     def do_start2():
         start_rows("o")
-        start_cols("s")
-        start_cols("f")
+        for g in "fsgt":
+            start_cols(g)
         start_rows("d")
         swap(0, r.tokens, r.tok.at[pl.ds(OWN, OWN)])
         swap(1, r.cot_in, r.cot.at[pl.ds(OWN, OWN)])
@@ -672,30 +681,34 @@
         swapped(0, r.tok.at[pl.ds(OWN, OWN)])
         over(0, OWN, lambda start: norm_rows(start, OWN, r.rg))
 
-    def do_proj():
+    def do_proj(part):
+        if part:
+            tile_loop(HALF, 256, lambda at, width: proj(at, width, 2 * HALF))
+            tile_loop(HALF, 256, proj_gate)
+            return
         unit_row = lax.broadcasted_iota(jnp.int32, (8, 128), 0)
         unit = jnp.where(unit_row == lax.broadcasted_iota(jnp.int32, (8, 128), 1), 1.0, 0.0).astype(BF16)
-        r.gain[...] = dot_t(unit, r.wa[:, pl.ds(4 * HALF, 128)])
+        r.gain[...] = dot_t(unit, r.wa[:, pl.ds(1024, 128)])
         row_loop(OWN, 64, gain_rows)
-        tile_loop(3 * HALF, 256, proj)
-        tile_loop(HALF, 256, proj_gate)
+        tile_loop(2 * HALF, 256, proj)
 
     def do_out(start):
-        if start == 0:
-            partial_rows(r.mix, out_product, 0, 0, 256)
-            return
         partial_rows(r.mix, out_product, 0, start, 128)
-        swap_rows(2 if start == 256 else 3, r.es.at[0], r.er.at[0], start - OWN, 128)
+        if start >= OWN:
+            swap_rows(2 if start == 256 else 3, r.es.at[0], r.er.at[0], start - OWN, 128)
 
     def do_resid(start):
         swapped_rows(2 + start // 128, r.er.at[0], start, 128)
         over(start, 128, resid_rows)
         swap(4 + start // 128, r.nt.at[pl.ds(start, 128)], r.nt.at[pl.ds(OWN + start, 128)])
 
-    def do_hidden():
+    def do_hidden(part):
+        if part:
+            tile_loop(640, 256, lambda at, width: hidden(at + 768, width))
+            return
         swapped(4, r.nt.at[pl.ds(OWN, 128)])
         swapped(5, r.nt.at[pl.ds(OWN + 128, 128)])
-        tile_loop(FH, 256, hidden)
+        tile_loop(768, 256, hidden)
 
     def do_cot():
         load_cot.wait()
@@ -768,32 +781,35 @@
         over(start, 64, attend_grad)
 
     work = (
-        (do_start,), (own, GA), (own, GB), (do_start2,), (got_y, GA, 0), (own, GO), (got_z, GA, 1, 0),
-        (got_z, GA, 2, 0), (got_y, GB, 0), (got_z, GO, 1, 0), (got_z, GB, 1, 0), (got_z, GO, 2, 0), (do_norm_own,),
-        (got_z, GO, 3, 0), (got_z, GB, 2, 0), (got_z, GA, 3, 0), (got_z, GB, 3, 0), (got_y, GO, 1), (got_y, GO, 0),
-        (got_y, GO, 3), (own, GF), (do_norm_partner,), (got_y, GB, 2), (got_y, GA, 1), (got_y, GB, 1), (own, GD),
-        (own, GS), (got_z, GF, 1, 0), (got_y, GA, 3), (got_y, GA, 2), (got_y, GO, 2), (got_y, GB, 3), (whole, GB),
-        (whole, GA), (do_proj,), (got_z, GS, 1, 0), (do_attend, 0), (do_attend, 320), (got_y, GD, 0),
-        (do_attend, 256), (whole, GO), (got_z, GS, 2, 0), (do_attend, 448), (do_out, 256), (do_attend, 384),
-        (got_y, GF, 0), (got_z, GF, 2, 0), (got_z, GD, 1, 0), (do_attend, 64), (do_attend, 192), (got_z, GD, 2, 0),
-        (got_y, GS, 0), (got_y, GF, 1), (do_out, 384), (got_z, GS, 3, 0), (got_z, GD, 1, 1), (got_y, GS, 1),
-        (do_attend, 128), (got_y, GS, 2), (do_out, 0), (do_resid, 0), (got_z, GF, 3, 0), (do_resid, 128),
-        (got_y, GF, 2), (got_z, GD, 3, 0), (got_z, GD, 2, 1), (got_y, GS, 3), (got_y, GF, 3), (whole, GS),
-        (got_z, GD, 3, 1), (whole, GF), (do_hidden,), (do_cot,), (give, 0), (give, 1), (whole, GD), (do_hidden_grad,),
-        (take, 0), (do_back, 256), (take, 1), (give, 2), (do_back, 384), (take, 2), (do_back, 0), (give, 3),
-        (do_resid_grad, 0), (pass_far, 1), (give, 4), (take_y, 0), (do_resid_grad, 128), (take, 3),
-        (do_mixed_grad, 0), (owner_sum, 1), (do_attend_grad, 0), (take_y, 2), (pass_far, 0), (do_attend_grad, 64),
-        (give, 5), (take, 4), (do_attend_grad, 192), (do_attend_grad, 128), (do_mixed_grad, 256),
-        (do_mixed_grad, 384), (give, 6), (take_y, 3), (pass_far, 2), (do_attend_grad, 448), (take, 5), (give, 7),
-        (do_attend_grad, 256), (do_take_z, 0), (do_attend_grad, 384), (take, 7), (do_attend_grad, 320),
-        (do_heads_back, 256), (pass_far, 3), (do_take_z, 1), (pass_far, 7), (do_heads_back, 0), (take, 6),
-        (take_y, 4), (give, 8), (do_block_out,), (take_y, 5), (take, 8), (give, 9), (give, 10), (pass_far, 4),
-        (do_tokens_grad,), (do_gsum, 0), (take, 9), (do_take_z, 2), (owner_sum, 7), (take_y, 6), (take_y, 8),
-        (pass_far, 5), (do_take_z, 4), (do_take_z, 3), (finish, 0), (take, 10), (pass_far, 8), (do_gsum, 1),
-        (pass_far, 6), (take_y, 9), (pass_far, 9), (finish, 2), (do_take_z, 6), (do_take_z, 7), (do_take_z, 5),
-        (take_y, 10), (finish, 1), (finish, 4), (pass_far, 10), (do_take_z, 9), (do_gsum, 2), (finish, 6),
-        (do_take_z, 8), (do_gsum, 3), (do_take_z, 10), (finish, 7), (finish, 8), (finish, 5), (finish, 3),
-        (finish, 9), (do_block_rows,), (finish, 10), (do_gsum, 4),
+        (do_start,), (own, GA), (own, GB), (do_start2,), (got_z, GA, 1, 0), (own, GO), (got_z, GA, 2, 0),
+        (got_z, GB, 1, 0), (do_norm_own,), (got_z, GB, 2, 0), (got_z, GA, 3, 0), (got_y, GO, 0), (got_z, GB, 3, 0),
+        (got_y, GA, 0), (got_z, GO, 1, 0), (got_z, GO, 2, 0), (got_z, GO, 3, 0), (got_y, GB, 0), (got_y, GA, 2),
+        (own, GS), (got_y, GB, 1), (own, GG), (own, GT), (got_y, GA, 3), (got_y, GB, 2), (own, GD), (got_y, GA, 1),
+        (own, GF), (do_norm_partner,), (got_z, GS, 1, 0), (whole, GA), (got_y, GB, 3), (do_proj, 0), (whole, GB),
+        (do_proj, 1), (got_y, GO, 1), (got_y, GO, 2), (got_y, GO, 3), (got_z, GG, 1, 0), (do_attend, 256),
+        (got_y, GS, 0), (whole, GO), (do_attend, 320), (do_out, 256), (got_z, GG, 2, 0), (got_z, GF, 1, 0),
+        (do_attend, 384), (do_attend, 448), (do_out, 384), (got_z, GF, 2, 0), (do_attend, 128), (got_z, GS, 1, 1),
+        (got_z, GS, 2, 1), (do_attend, 192), (got_z, GG, 3, 0), (do_attend, 64), (do_attend, 0), (do_out, 0),
+        (do_out, 128), (got_z, GF, 3, 0), (do_resid, 0), (got_y, GD, 0), (got_z, GS, 3, 1), (got_z, GT, 1, 0),
+        (got_z, GT, 2, 0), (got_z, GT, 3, 0), (got_y, GT, 0), (got_z, GS, 2, 0), (got_y, GG, 0), (got_z, GD, 1, 0),
+        (do_resid, 128), (got_z, GD, 2, 0), (got_y, GG, 2), (got_z, GS, 3, 0), (whole, GS), (got_y, GF, 3),
+        (got_y, GG, 3), (got_y, GG, 1), (got_y, GF, 2), (got_y, GT, 1), (got_y, GF, 0), (got_y, GF, 1), (whole, GG),
+        (whole, GF), (got_y, GT, 2), (got_z, GD, 3, 0), (got_y, GT, 3), (do_hidden, 0), (whole, GT), (do_hidden, 1),
+        (do_cot,), (give, 0), (give, 1), (got_y, GD, 1), (got_y, GD, 2), (take, 0), (got_y, GD, 3), (take, 1),
+        (whole, GD), (do_hidden_grad,), (give, 2), (do_back, 256), (give, 3), (take, 2), (give, 4), (take, 3),
+        (give, 5), (do_back, 384), (take_y, 0), (take, 5), (pass_far, 1), (do_back, 0), (do_resid_grad, 0),
+        (take_y, 2), (do_resid_grad, 128), (pass_far, 0), (do_mixed_grad, 0), (do_attend_grad, 64), (owner_sum, 1),
+        (do_attend_grad, 128), (do_attend_grad, 0), (do_attend_grad, 192), (take, 4), (do_mixed_grad, 256),
+        (pass_far, 2), (do_attend_grad, 320), (do_take_z, 0), (take_y, 3), (do_take_z, 2), (do_attend_grad, 256),
+        (do_mixed_grad, 384), (do_attend_grad, 384), (do_attend_grad, 448), (give, 6), (pass_far, 3), (take_y, 5),
+        (do_heads_back, 256), (give, 7), (take, 6), (give, 8), (do_take_z, 1), (take, 7), (give, 9), (take, 8),
+        (pass_far, 5), (give, 10), (take, 10), (pass_far, 7), (do_take_z, 5), (take_y, 4), (do_take_z, 3),
+        (do_heads_back, 0), (do_tokens_grad,), (do_gsum, 0), (take, 9), (do_block_out,), (take_y, 6), (pass_far, 4),
+        (do_take_z, 4), (take_y, 8), (finish, 1), (pass_far, 6), (do_take_z, 6), (take_y, 10), (pass_far, 8),
+        (owner_sum, 7), (take_y, 9), (do_gsum, 1), (pass_far, 10), (finish, 4), (do_take_z, 8), (pass_far, 9),
+        (do_gsum, 2), (do_take_z, 10), (do_take_z, 7), (finish, 0), (finish, 2), (do_gsum, 3), (do_take_z, 9),
+        (finish, 10), (do_block_rows,), (finish, 6), (finish, 3), (finish, 5), (finish, 8), (finish, 7), (do_gsum, 4),
+        (finish, 9),
     )
     for step, *args in work:
         step(*args)
@@ -803,7 +819,7 @@
         pl.when(pred)(copy.wait_send)
     for copy in finals + outs:
         copy.wait()
-    for g in "abfs":
+    for g in SPANS:
         gi = GROUPS.index(g)
         own = col_shard(g, x)
         remote(own, own, r.s_xs.at[gi, 0], r.s_xs.at[gi, 0], xn).wait_send()
@@ -841,7 +857,6 @@
 def fused_layer(
     tokens, attn_gain, w_query, w_key, w_value, w_gate, w_output, ffn_gain, w_first, w_second, w_down, cotangent
 ):
-    gains = jnp.pad(jnp.stack([attn_gain, ffn_gain], axis=1), ((0, 0), (0, 126)))
     items = scratch_list()
     names = IN_NAMES + OUT_NAMES + tuple(name for name, _ in items)
     shape = jax.ShapeDtypeStruct
@@ -852,12 +867,12 @@
             shape((32, D), F32), shape((32, D), F32), shape((32, D), F32), shape((32, D), F32), shape((32, D), F32),
             shape((32, FF), F32), shape((32, FF), F32), shape((88, D), F32),
         ],
-        in_specs=[pl.BlockSpec(memory_space=pl.ANY)] * len(IN_NAMES),
+        in_specs=[pl.BlockSpec(memory_space=pltpu.VMEM if n.startswith("gain") else pl.ANY) for n in IN_NAMES],
         out_specs=[pl.BlockSpec(memory_space=pl.ANY)] * len(OUT_NAMES),
         scratch_shapes=[spec for _, spec in items],
         compiler_params=pltpu.CompilerParams(collective_id=0, has_side_effects=True, vmem_limit_bytes=66 * 2**20 - 2**21),
         name="layer",
-    )(tokens, gains, w_query, w_key, w_value, w_gate, w_output, w_first, w_second, w_down, cotangent)
+    )(tokens, attn_gain, ffn_gain, w_query, w_key, w_value, w_gate, w_output, w_first, w_second, w_down, cotangent)
     block_out, tokens_grad, gain_grads, gq, gk, gv, gg, go, g1, g2, gd = outs
     kept = (block_out, tokens_grad, gq, gk, gv, gg, go, g1, g2, gd)
     anywhere = pl.BlockSpec(memory_space=pl.ANY)

time: 181 us -> 176 us (0.972)
  Pallas kernels: 178 us -> 175 us
    pallas_call x1, Pallas kernels: 174 us -> 171 us  [fused_layer(): pl.pallas_call(functools.partial(layer_kernel, names), out_shape=[shape((...]
where the time goes in v4:
time: 176 us
  Pallas kernels  175 us (99%)
    pallas_call x1, Pallas kernels, fused_layer(): pl.pallas_call(functools.partial(layer_kernel, names), out_shape=[shape((...  171 us
    pallas_call x1, Pallas kernels, fused_layer(): pl.pallas_call(hand_over, out_shape=[shape((32,), F32)] * 2 + [shape(v.sh...  4.38 us

profile of v4, /device:TPU:0, one launch (start us, length us, event | category | flops | bytes accessed | tf_op | source)
XLA Modules:
  0.0 176.1 jit_solution(4494334700403782874)
XLA Ops:
  0.6 170.9 %layer.1 = (bf16[256,1024]{1,0:T(8,128)(2,1)}, f32[256,1024]{1,0:T(8,128)}, f32[8,1024]{1,0:T(8,128)}, f32[32,1024]{1,0:T(8,128)}, f32[32,1024]{1,0:T(8,128)}, /...) custom-call(bf16[256,1024]{1,0:T(8,128)(2,1)} %refs_0_.1, ...), custom_call_target="tpu_custom_call" | custom-call | tf_op jit(solution)/shard_map/layer/pallas_call | solution.py:863
  171.6 4.4 %hand_over.1 = (f32[32]{0:T(128)}, f32[32]{0:T(128)}, bf16[256,1024]{1,0:T(8,128)(2,1)}, f32[256,1024]{1,0:T(8,128)}, f32[32,1024]{1,0:T(8,128)}, /*index=5*/f32...) custom-call(f32[8,1024]{1,0:T(8,128)} %get-tuple-element.35.gain_ref, ...), custom_call_target="tpu_custom_call" | custom-call | tf_op jit(solution)/shard_map/hand_over/pallas_call | solution.py:880

commit v5 on v4

--- a/solution.py
+++ b/solution.py
@@ -28,14 +28,14 @@
     ("d", 0, 256), ("d", 256, 256),
     ("f", 0, 768), ("f", 768, 640), ("f", 1408, 768), ("f", 2176, 640),
     ("o", 0, 512),
-    ("a", 1536, 512), ("a", 1024, 512), ("a", 512, 512), ("a", 0, 512),
+    ("a", 1536, 512), ("a", 1024, 512), ("a", 512, 512), ("a", 0, 256), ("a", 256, 256),
 )
 NCH = len(CHUNKS)
 Z_FIRST = tuple(i in (1, 7,) for i in range(NCH))
 Y_FIRST = ("s",)
-GROUPS = ("a", "b", "o", "f", "s", "g", "t", "d")
-GA, GB, GO, GF, GS, GG, GT, GD = GROUPS
-SPANS = {"a": (0, 1152), "b": (1152, 1024), "f": (0, 768), "g": (768, 640), "s": (FH, 768), "t": (FH + 768, 640)}
+GROUPS = ("h", "a", "b", "o", "f", "s", "g", "t", "d")
+GH, GA, GB, GO, GF, GS, GG, GT, GD = GROUPS
+SPANS = {"h": (0, 1152), "a": (0, 1152), "b": (1152, 1024), "f": (0, 768), "g": (768, 640), "s": (FH, 768), "t": (FH + 768, 640)}
 
 
 def piece_rows(kind):
@@ -174,8 +174,11 @@
     m = z * 2 + y
 
     def piece(g, cc, zz, yy):
+        if g in "ha":
+            part = x if g == "h" else 1 - x
+            return r.wa.at[rows_of(64 * (cc * 8 + zz * 2 + yy) + 32 * part, 32, 32), pl.ds(*SPANS[g])]
         if g in SPANS:
-            full = r.wa if g in "ab" else r.wf
+            full = r.wa if g == "b" else r.wf
             return full.at[rows_of(64 * (cc * 8 + zz * 2 + yy), 64, 64), pl.ds(*SPANS[g])]
         if g == "o":
             return r.wo.at[rows_of(64 * (zz * 2 + yy), 64, 64), lanes_of(512 * cc, 512)]
@@ -183,7 +186,7 @@
 
     def col_shard(g, who):
         row = rows_of(64 * p + 32 * who, 32, 32)
-        return (r.wa if g in "ab" else r.wf).at[row, pl.ds(*SPANS[g])]
+        return (r.wa if g in "hab" else r.wf).at[row, pl.ds(*SPANS[g])]
 
     def start_cols(g):
         gi = GROUPS.index(g)
@@ -231,10 +234,13 @@
 
     def piece_ready(g):
         gi = GROUPS.index(g)
-        if g in SPANS:
+        if g == "a":
+            arrived(col_shard(g, 1 - x), r.s_xr.at[gi])
+        elif g in SPANS:
             own = col_shard(g, x)
-            pltpu.make_async_copy(own, own, r.s_wl.at[gi]).wait()
-            arrived(col_shard(g, 1 - x), r.s_xr.at[gi])
+            pltpu.make_async_copy(own, own, r.s_wl.at[GROUPS.index("a") if g == "h" else gi]).wait()
+            if g != "h":
+                arrived(col_shard(g, 1 - x), r.s_xr.at[gi])
         elif g == "o":
             arrived(piece("o", c, z, y), r.s_xr.at[gi])
         else:
@@ -598,7 +604,7 @@
             if kind == "f":
                 out, place = (r.g1, FH * x + at) if at < FH else (r.g2, FH * x + at - FH)
             else:
-                out, place = (r.gq, r.gk, r.gv, r.gg)[at // 512], HALF * x
+                out, place = (r.gq, r.gk, r.gv, r.gg)[at // 512], HALF * x + at % 512
             dst = out.at[:, lanes_of(place, cols)]
             finals.append(local(fin.at[rows_of(32 * x, 32, 32)], dst, r.r_fs.at[i, 0]))
             send(fin.at[rows_of(32 * (1 - x), 32, 32)], dst, r.r_fs.at[i, 1], r.r_fr.at[i, 0], xn)
@@ -624,7 +630,7 @@
             if kind == "f":
                 out, place = (r.g1, FH * (1 - x) + at) if at < FH else (r.g2, FH * (1 - x) + at - FH)
             else:
-                out, place = (r.gq, r.gk, r.gv, r.gg)[at // 512], HALF * (1 - x)
+                out, place = (r.gq, r.gk, r.gv, r.gg)[at // 512], HALF * (1 - x) + at % 512
             arrived(out.at[:, lanes_of(place, cols)], r.r_fr.at[i, 0])
             return
         out = r.gd if kind == "d" else r.go
@@ -781,35 +787,37 @@
         over(start, 64, attend_grad)
 
     work = (
-        (do_start,), (own, GA), (own, GB), (do_start2,), (got_z, GA, 1, 0), (own, GO), (got_z, GA, 2, 0),
-        (got_z, GB, 1, 0), (do_norm_own,), (got_z, GB, 2, 0), (got_z, GA, 3, 0), (got_y, GO, 0), (got_z, GB, 3, 0),
-        (got_y, GA, 0), (got_z, GO, 1, 0), (got_z, GO, 2, 0), (got_z, GO, 3, 0), (got_y, GB, 0), (got_y, GA, 2),
-        (own, GS), (got_y, GB, 1), (own, GG), (own, GT), (got_y, GA, 3), (got_y, GB, 2), (own, GD), (got_y, GA, 1),
-        (own, GF), (do_norm_partner,), (got_z, GS, 1, 0), (whole, GA), (got_y, GB, 3), (do_proj, 0), (whole, GB),
-        (do_proj, 1), (got_y, GO, 1), (got_y, GO, 2), (got_y, GO, 3), (got_z, GG, 1, 0), (do_attend, 256),
-        (got_y, GS, 0), (whole, GO), (do_attend, 320), (do_out, 256), (got_z, GG, 2, 0), (got_z, GF, 1, 0),
-        (do_attend, 384), (do_attend, 448), (do_out, 384), (got_z, GF, 2, 0), (do_attend, 128), (got_z, GS, 1, 1),
-        (got_z, GS, 2, 1), (do_attend, 192), (got_z, GG, 3, 0), (do_attend, 64), (do_attend, 0), (do_out, 0),
-        (do_out, 128), (got_z, GF, 3, 0), (do_resid, 0), (got_y, GD, 0), (got_z, GS, 3, 1), (got_z, GT, 1, 0),
-        (got_z, GT, 2, 0), (got_z, GT, 3, 0), (got_y, GT, 0), (got_z, GS, 2, 0), (got_y, GG, 0), (got_z, GD, 1, 0),
-        (do_resid, 128), (got_z, GD, 2, 0), (got_y, GG, 2), (got_z, GS, 3, 0), (whole, GS), (got_y, GF, 3),
-        (got_y, GG, 3), (got_y, GG, 1), (got_y, GF, 2), (got_y, GT, 1), (got_y, GF, 0), (got_y, GF, 1), (whole, GG),
-        (whole, GF), (got_y, GT, 2), (got_z, GD, 3, 0), (got_y, GT, 3), (do_hidden, 0), (whole, GT), (do_hidden, 1),
-        (do_cot,), (give, 0), (give, 1), (got_y, GD, 1), (got_y, GD, 2), (take, 0), (got_y, GD, 3), (take, 1),
-        (whole, GD), (do_hidden_grad,), (give, 2), (do_back, 256), (give, 3), (take, 2), (give, 4), (take, 3),
-        (give, 5), (do_back, 384), (take_y, 0), (take, 5), (pass_far, 1), (do_back, 0), (do_resid_grad, 0),
-        (take_y, 2), (do_resid_grad, 128), (pass_far, 0), (do_mixed_grad, 0), (do_attend_grad, 64), (owner_sum, 1),
-        (do_attend_grad, 128), (do_attend_grad, 0), (do_attend_grad, 192), (take, 4), (do_mixed_grad, 256),
-        (pass_far, 2), (do_attend_grad, 320), (do_take_z, 0), (take_y, 3), (do_take_z, 2), (do_attend_grad, 256),
-        (do_mixed_grad, 384), (do_attend_grad, 384), (do_attend_grad, 448), (give, 6), (pass_far, 3), (take_y, 5),
-        (do_heads_back, 256), (give, 7), (take, 6), (give, 8), (do_take_z, 1), (take, 7), (give, 9), (take, 8),
-        (pass_far, 5), (give, 10), (take, 10), (pass_far, 7), (do_take_z, 5), (take_y, 4), (do_take_z, 3),
-        (do_heads_back, 0), (do_tokens_grad,), (do_gsum, 0), (take, 9), (do_block_out,), (take_y, 6), (pass_far, 4),
-        (do_take_z, 4), (take_y, 8), (finish, 1), (pass_far, 6), (do_take_z, 6), (take_y, 10), (pass_far, 8),
-        (owner_sum, 7), (take_y, 9), (do_gsum, 1), (pass_far, 10), (finish, 4), (do_take_z, 8), (pass_far, 9),
-        (do_gsum, 2), (do_take_z, 10), (do_take_z, 7), (finish, 0), (finish, 2), (do_gsum, 3), (do_take_z, 9),
-        (finish, 10), (do_block_rows,), (finish, 6), (finish, 3), (finish, 5), (finish, 8), (finish, 7), (do_gsum, 4),
-        (finish, 9),
+        (do_start,), (own, GH), (own, GA), (got_z, GH, 1, 0), (own, GB), (do_start2,), (got_z, GH, 2, 0),
+        (got_y, GA, 0), (got_z, GA, 1, 0), (own, GO), (got_z, GA, 2, 0), (got_y, GH, 1), (got_y, GH, 0),
+        (do_norm_own,), (got_z, GB, 1, 0), (got_z, GB, 2, 0), (got_z, GH, 3, 0), (got_z, GA, 3, 0), (got_y, GO, 0),
+        (got_z, GB, 3, 0), (got_y, GA, 2), (got_y, GH, 2), (got_z, GO, 1, 0), (got_z, GO, 2, 0), (got_y, GB, 1),
+        (got_z, GO, 3, 0), (own, GS), (own, GF), (got_y, GB, 2), (got_y, GA, 3), (got_y, GB, 0), (got_y, GH, 3),
+        (own, GD), (got_y, GA, 1), (own, GT), (own, GG), (do_norm_partner,), (whole, GH), (got_y, GB, 3), (whole, GA),
+        (do_proj, 0), (whole, GB), (do_proj, 1), (got_y, GO, 2), (got_y, GO, 1), (got_y, GO, 3), (got_z, GS, 1, 0),
+        (do_attend, 256), (whole, GO), (do_attend, 320), (do_out, 256), (got_z, GT, 1, 0), (do_attend, 448),
+        (got_z, GF, 1, 0), (got_z, GG, 1, 0), (got_z, GF, 2, 0), (got_z, GS, 2, 0), (got_z, GG, 2, 0),
+        (do_attend, 384), (got_y, GD, 0), (got_y, GS, 0), (do_out, 384), (got_z, GS, 3, 0), (do_attend, 0),
+        (do_attend, 64), (do_out, 0), (do_resid, 0), (got_z, GF, 3, 0), (got_z, GG, 3, 0), (got_y, GT, 1),
+        (do_attend, 192), (got_z, GT, 2, 0), (got_y, GT, 0), (got_z, GS, 1, 1), (got_z, GS, 2, 1), (got_y, GG, 0),
+        (got_z, GT, 3, 0), (do_attend, 128), (got_z, GD, 1, 0), (do_out, 128), (do_resid, 128), (got_y, GG, 1),
+        (got_z, GD, 2, 0), (got_y, GG, 2), (got_z, GS, 3, 1), (whole, GS), (got_y, GG, 3), (got_y, GF, 3),
+        (got_y, GF, 1), (got_y, GF, 2), (got_y, GF, 0), (whole, GG), (whole, GF), (got_y, GT, 2), (got_z, GD, 3, 0),
+        (got_y, GT, 3), (do_hidden, 0), (whole, GT), (do_hidden, 1), (do_cot,), (give, 0), (give, 1), (got_y, GD, 2),
+        (got_y, GD, 1), (take, 0), (got_y, GD, 3), (take, 1), (whole, GD), (do_hidden_grad,), (give, 2),
+        (do_back, 256), (give, 3), (take, 2), (give, 4), (take, 3), (give, 5), (pass_far, 1), (take_y, 0),
+        (do_back, 384), (take, 5), (do_back, 0), (do_resid_grad, 0), (take_y, 2), (do_resid_grad, 128),
+        (do_mixed_grad, 0), (do_attend_grad, 64), (do_attend_grad, 192), (do_attend_grad, 0), (pass_far, 0),
+        (do_mixed_grad, 256), (do_attend_grad, 320), (take_y, 3), (do_take_z, 0), (pass_far, 2), (take, 4),
+        (do_mixed_grad, 384), (give, 6), (do_attend_grad, 448), (do_attend_grad, 256), (pass_far, 3), (take_y, 5),
+        (give, 7), (do_attend_grad, 128), (do_take_z, 2), (do_attend_grad, 384), (do_heads_back, 256), (take, 6),
+        (give, 8), (take, 7), (give, 9), (pass_far, 5), (take, 9), (take, 8), (give, 10), (give, 11), (take, 11),
+        (pass_far, 7), (take_y, 4), (do_take_z, 3), (owner_sum, 1), (do_heads_back, 0), (do_block_out,),
+        (do_tokens_grad,), (do_gsum, 0), (take_y, 9), (do_take_z, 5), (pass_far, 4), (do_take_z, 4), (take_y, 6),
+        (take, 10), (finish, 0), (pass_far, 9), (take_y, 11), (owner_sum, 7), (take_y, 8), (do_take_z, 1),
+        (do_take_z, 9), (finish, 2), (pass_far, 6), (pass_far, 11), (do_block_rows,), (do_gsum, 1), (pass_far, 8),
+        (do_take_z, 6), (finish, 4), (take_y, 10), (do_take_z, 7), (do_gsum, 2), (finish, 3), (pass_far, 10),
+        (finish, 9), (do_gsum, 3), (do_take_z, 8), (do_take_z, 11), (finish, 1), (finish, 6), (do_take_z, 10),
+        (finish, 5), (finish, 10), (finish, 8), (finish, 7), (finish, 11), (do_gsum, 4),
     )
     for step, *args in work:
         step(*args)
@@ -819,7 +827,7 @@
         pl.when(pred)(copy.wait_send)
     for copy in finals + outs:
         copy.wait()
-    for g in SPANS:
+    for g in "abfsgt":
         gi = GROUPS.index(g)
         own = col_shard(g, x)
         remote(own, own, r.s_xs.at[gi, 0], r.s_xs.at[gi, 0], xn).wait_send()

time: 176 us -> 172 us (0.977)
  Pallas kernels: 175 us -> 171 us
    pallas_call x1, Pallas kernels: 171 us -> 167 us  [fused_layer(): pl.pallas_call(functools.partial(layer_kernel, names), out_shape=[shape((...]
where the time goes in v5:
time: 172 us
  Pallas kernels  171 us (99%)
    pallas_call x1, Pallas kernels, fused_layer(): pl.pallas_call(functools.partial(layer_kernel, names), out_shape=[shape((...  167 us
    pallas_call x1, Pallas kernels, fused_layer(): pl.pallas_call(hand_over, out_shape=[shape((32,), F32)] * 2 + [shape(v.sh...  4.38 us

profile of v5, /device:TPU:0, one launch (start us, length us, event | category | flops | bytes accessed | tf_op | source)
XLA Modules:
  0.0 172.0 jit_solution(11912872861360030282)
XLA Ops:
  0.6 166.8 %layer.1 = (bf16[256,1024]{1,0:T(8,128)(2,1)}, f32[256,1024]{1,0:T(8,128)}, f32[8,1024]{1,0:T(8,128)}, f32[32,1024]{1,0:T(8,128)}, f32[32,1024]{1,0:T(8,128)}, /...) custom-call(bf16[256,1024]{1,0:T(8,128)(2,1)} %refs_0_.1, ...), custom_call_target="tpu_custom_call" | custom-call | tf_op jit(solution)/shard_map/layer/pallas_call | solution.py:871
  167.5 4.4 %hand_over.1 = (f32[32]{0:T(128)}, f32[32]{0:T(128)}, bf16[256,1024]{1,0:T(8,128)(2,1)}, f32[256,1024]{1,0:T(8,128)}, f32[32,1024]{1,0:T(8,128)}, /*index=5*/f32...) custom-call(f32[8,1024]{1,0:T(8,128)} %get-tuple-element.35.gain_ref, ...), custom_call_target="tpu_custom_call" | custom-call | tf_op jit(solution)/shard_map/hand_over/pallas_call | solution.py:888

commit v6 on v5

--- a/solution.py
+++ b/solution.py
@@ -327,24 +327,24 @@
 
     def grad_sum(n, value=None):
         def out(slot, to):
-            send(r.gs.at[min(slot, 3)], r.gr.at[slot], r.s_gs.at[slot], r.s_gr.at[slot], to)
+            send(r.gs.at[min(slot, 3), pl.ds(0, 2)], r.gr.at[slot, pl.ds(0, 2)], r.s_gs.at[slot], r.s_gr.at[slot], to)
 
         def got(slot):
-            arrived(r.gr.at[slot], r.s_gr.at[slot])
-            return r.gr[slot]
+            arrived(r.gr.at[slot, pl.ds(0, 2)], r.s_gr.at[slot])
+            return r.gr[slot, 0:2, :]
 
         if n == 0:
             r.gs[0] = value
             out(0, xn)
         elif n < 3:
-            r.gs[n] = r.gs[n - 1] + got(n - 1)
+            r.gs[n, 0:2, :] = r.gs[n - 1, 0:2, :] + got(n - 1)
             out(n, yn if n == 1 else sib)
         elif n == 3:
-            r.gs[3] = r.gs[2] + got(2)
+            r.gs[3, 0:2, :] = r.gs[2, 0:2, :] + got(2)
             for k in (1, 2, 3):
-                send(r.gs.at[3], r.gr.at[6 - k], r.s_gs.at[2 + k], r.s_gr.at[6 - k], zp[k])
+                send(r.gs.at[3, pl.ds(0, 2)], r.gr.at[6 - k, pl.ds(0, 2)], r.s_gs.at[2 + k], r.s_gr.at[6 - k], zp[k])
         else:
-            return r.gs[3] + (got(3) + got(4) + got(5))
+            return r.gs[3, 0:2, :] + (got(3) + got(4) + got(5))
 
     def norm_rows(start, at, out):
         v = r.tok[pl.ds(start + at, 64), :].astype(F32)
@@ -769,7 +769,7 @@
         elif n < 4:
             grad_sum(n)
         else:
-            r.gacc[0] = grad_sum(4)
+            r.gacc[0, 0:2, :] = grad_sum(4)
             outs.append(local(r.gacc.at[0], r.gain_grads, r.s_out.at[2]))
 
     def do_take_z(i):

time: 172 us -> 172 us (level)
  no operation moved by 1% of the time
where the time goes in v6:
time: 172 us
  Pallas kernels  171 us (99%)
    pallas_call x1, Pallas kernels, fused_layer(): pl.pallas_call(functools.partial(layer_kernel, names), out_shape=[shape((...  167 us
    pallas_call x1, Pallas kernels, fused_layer(): pl.pallas_call(hand_over, out_shape=[shape((32,), F32)] * 2 + [shape(v.sh...  4.38 us

profile of v6, /device:TPU:0, one launch (start us, length us, event | category | flops | bytes accessed | tf_op | source)
XLA Modules:
  0.0 172.1 jit_solution(737668335948342884)
XLA Ops:
  0.6 166.8 %layer.1 = (bf16[256,1024]{1,0:T(8,128)(2,1)}, f32[256,1024]{1,0:T(8,128)}, f32[8,1024]{1,0:T(8,128)}, f32[32,1024]{1,0:T(8,128)}, f32[32,1024]{1,0:T(8,128)}, /...) custom-call(bf16[256,1024]{1,0:T(8,128)(2,1)} %refs_0_.1, ...), custom_call_target="tpu_custom_call" | custom-call | tf_op jit(solution)/shard_map/layer/pallas_call | solution.py:871
  167.5 4.4 %hand_over.1 = (f32[32]{0:T(128)}, f32[32]{0:T(128)}, bf16[256,1024]{1,0:T(8,128)(2,1)}, f32[256,1024]{1,0:T(8,128)}, f32[32,1024]{1,0:T(8,128)}, /*index=5*/f32...) custom-call(f32[8,1024]{1,0:T(8,128)} %get-tuple-element.35.gain_ref, ...), custom_call_target="tpu_custom_call" | custom-call | tf_op jit(solution)/shard_map/hand_over/pallas_call | solution.py:888
